TPU v7x, 32 devices: a whole 2x2x4 slice. The times are simulated.
32 devices in a mesh: scene: 2 (over x), seq: 16 (over z, y, core).
Axes of the slice: x: 2, y: 2, z: 4, core: 2. Of those that a mesh axis runs over, the one named last changes fastest.
Arguments:
- tokens: bfloat16 [2, 4096, 1024], P('scene', 'seq'), may hold values from -6 to 6
- surface_mask: int32 [2, 4096], P('scene', 'seq'), may hold values 0 or 1
- out_grad: bfloat16 [2, 4096, 1024], P('scene', 'seq'), may hold values from -6 to 6
- w_query: bfloat16 [1024, 1024], replicated, may hold values from -0.1875 to 0.1875
- w_key: bfloat16 [1024, 1024], replicated, may hold values from -0.1875 to 0.1875
- w_value: bfloat16 [1024, 1024], replicated, may hold values from -0.1875 to 0.1875
- w_out: bfloat16 [1024, 1024], replicated, may hold values from -6 to 6
- w_up: bfloat16 [1024, 4096], replicated, may hold values from -0.1875 to 0.1875
- w_down: bfloat16 [4096, 1024], replicated, may hold values from -0.09375 to 0.09375
- b_query: float32 [1024], replicated, may hold values from -3 to 3
- b_value: float32 [1024], replicated, may hold values from -3 to 3
- b_out: float32 [1024], replicated, may hold values from -3 to 3
- b_up: float32 [4096], replicated, may hold values from -3 to 3
- b_down: float32 [1024], replicated, may hold values from -3 to 3
- gain_one: float32 [1024], replicated, may hold values from 0.1 to 1.9
- shift_one: float32 [1024], replicated, may hold values from -3 to 3
- gain_two: float32 [1024], replicated, may hold values from 0.1 to 1.9
- shift_two: float32 [1024], replicated, may hold values from -3 to 3
Outputs:
- block_out: bfloat16 [2, 4096, 1024], P('scene', 'seq')
- tokens_grad: bfloat16 [2, 4096, 1024], P('scene', 'seq')
- query_grad: float32 [1024, 1024], P(('scene', 'seq'))
- key_grad: float32 [1024, 1024], P(('scene', 'seq'))
- value_grad: float32 [1024, 1024], P(('scene', 'seq'))
- out_proj_grad: float32 [1024, 1024], P(('scene', 'seq'))
- up_grad: float32 [1024, 4096], P(('scene', 'seq'))
- down_grad: float32 [4096, 1024], P(('scene', 'seq'))
- query_bias_grad: float32 [1024], P(('scene', 'seq'))
- value_bias_grad: float32 [1024], P(('scene', 'seq'))
- out_bias_grad: float32 [1024], P(('scene', 'seq'))
- up_bias_grad: float32 [4096], P(('scene', 'seq'))
- down_bias_grad: float32 [1024], P(('scene', 'seq'))
- gain_one_grad: float32 [1024], P(('scene', 'seq'))
- shift_one_grad: float32 [1024], P(('scene', 'seq'))
- gain_two_grad: float32 [1024], P(('scene', 'seq'))
- shift_two_grad: float32 [1024], P(('scene', 'seq'))
All inputs are finite; a program needn't handle non-finite values. No bound on the sum of `surface_mask` on one device may be relied on, other than what follows from the above.
Results may differ from a plain program's by a relative error of at most 0.014.
Values may be sent and summed in bfloat16 or wider, within the bound.
A program may use at most 320 MiB of HBM per device.

v0:
```python
import jax
import jax.numpy as jnp
from jax import lax
from jax.sharding import PartitionSpec as P

HEADS = 16
HEAD_DIM = 64


norm_eps = 1e-05
score_scale = 0.125
gelu_coef = 0.7978845608028654


def norm_rows(values, gain, shift):
    row_mean = jnp.mean(values, axis=-1, keepdims=True)
    centred = values - row_mean
    row_var = jnp.mean(centred * centred, axis=-1, keepdims=True)
    return centred * lax.rsqrt(row_var + norm_eps) * gain + shift


def gelu_tanh(values):
    return (
        0.5 * values * (1.0 + jnp.tanh(gelu_coef * (values + 0.044715 * values * values * values)))
    )


def matmul(left, right):
    return jnp.dot(left, right, preferred_element_type=jnp.float32)


def matmul_tn(left, right):
    return lax.dot_general(
        left, right, (((0,), (0,)), ((), ())), preferred_element_type=jnp.float32
    )


def matmul_nt(left, right):
    return lax.dot_general(
        left, right, (((1,), (1,)), ((), ())), preferred_element_type=jnp.float32
    )


def take_pair(array_in, pair_index):
    pair_width = 2 * HEAD_DIM
    sliced = lax.dynamic_slice_in_dim(array_in, pair_index * pair_width, pair_width, 2)
    return sliced.reshape(sliced.shape[:2] + (2, HEAD_DIM))


def take_stats(array_in, pair_index):
    return lax.dynamic_slice_in_dim(array_in, pair_index * 2, 2, 1)


def join_pairs(stacked):
    moved = jnp.moveaxis(stacked, 0, 2)
    return moved.reshape(moved.shape[:2] + (moved.shape[2] * moved.shape[3],))


def join_stats(stacked):
    moved = jnp.moveaxis(stacked, 0, 1)
    return moved.reshape((moved.shape[0], moved.shape[1] * moved.shape[2], moved.shape[3]))


def merge_heads(pair_part):
    return pair_part.reshape(pair_part.shape[:2] + (2 * HEAD_DIM,))


def attend(q_scene, k_gathered, v_gathered):

    def attend_pair_step(unused, pair_index):
        q_pair = take_pair(q_scene, pair_index)
        k_pair = take_pair(k_gathered, pair_index)
        v_pair = take_pair(v_gathered, pair_index)
        scores = (
            jnp.einsum("sqhe,skhe->shqk", q_pair, k_pair, preferred_element_type=jnp.float32)
            * score_scale
        )
        row_max = jnp.max(scores, axis=-1, keepdims=True)
        shifted = jnp.exp(scores - row_max)
        row_sum = jnp.sum(shifted, axis=-1, keepdims=True)
        prob_low = (shifted / row_sum).astype(jnp.bfloat16)
        pair_out = jnp.einsum(
            "shqk,skhe->sqhe", prob_low, v_pair, preferred_element_type=jnp.float32
        )
        pair_lse = (row_max + jnp.log(row_sum))[..., 0]
        return (unused, (merge_heads(pair_out), pair_lse))

    pair_count = HEADS // 2
    _, (pair_outs, pair_lses) = lax.scan(
        attend_pair_step, jnp.zeros((), jnp.float32), jnp.arange(pair_count, dtype=jnp.int32)
    )
    return (join_pairs(pair_outs), join_stats(pair_lses))


def query_side(q_scene, k_gathered, v_gathered, row_lse, att_grad):

    def query_pair_step(unused, pair_index):
        q_pair = take_pair(q_scene, pair_index)
        k_pair = take_pair(k_gathered, pair_index)
        v_pair = take_pair(v_gathered, pair_index)
        d_pair = take_pair(att_grad, pair_index)
        l_pair = take_stats(row_lse, pair_index)
        scores = (
            jnp.einsum("sqhe,skhe->shqk", q_pair, k_pair, preferred_element_type=jnp.float32)
            * score_scale
        )
        attn_prob = jnp.exp(scores - l_pair[..., None])
        dprob = jnp.einsum("sqhe,skhe->shqk", d_pair, v_pair, preferred_element_type=jnp.float32)
        row_delta = jnp.sum(attn_prob * dprob, axis=-1)
        dscore = (attn_prob * (dprob - row_delta[..., None])).astype(jnp.bfloat16)
        q_part = (
            jnp.einsum("shqk,skhe->sqhe", dscore, k_pair, preferred_element_type=jnp.float32)
            * score_scale
        )
        results = (merge_heads(q_part), row_delta)
        prob_low = attn_prob.astype(jnp.bfloat16)
        k_part = (
            jnp.einsum("shqk,sqhe->skhe", dscore, q_pair, preferred_element_type=jnp.float32)
            * score_scale
        )
        v_part = jnp.einsum("shqk,sqhe->skhe", prob_low, d_pair, preferred_element_type=jnp.float32)
        results = results + (merge_heads(k_part), merge_heads(v_part))
        return (unused, results)

    pair_count = HEADS // 2
    _, results = lax.scan(
        query_pair_step, jnp.zeros((), jnp.float32), jnp.arange(pair_count, dtype=jnp.int32)
    )
    return results


def on_device(
    tokens,
    surface_mask,
    out_grad,
    w_query,
    w_key,
    w_value,
    w_out,
    w_up,
    w_down,
    b_query,
    b_value,
    b_out,
    b_up,
    b_down,
    gain_one,
    shift_one,
    gain_two,
    shift_two,
):
    scenes, local_len, model_width = tokens.shape
    row_count = scenes * local_len
    flat_rows = tokens.astype(jnp.float32).reshape(row_count, model_width)
    normed, norm_one_pull = jax.vjp(norm_rows, flat_rows, gain_one, shift_one)
    normed_low = normed.astype(jnp.bfloat16)
    q_low = (matmul(normed_low, w_query) + b_query).astype(jnp.bfloat16)
    k_low = matmul(normed_low, w_key).astype(jnp.bfloat16)
    v_low = (matmul(normed_low, w_value) + b_value).astype(jnp.bfloat16)
    q_scene = q_low.reshape(scenes, local_len, model_width)
    k_scene = k_low.reshape(scenes, local_len, model_width)
    v_scene = v_low.reshape(scenes, local_len, model_width)
    k_gathered, v_gathered = (
        lax.all_gather(k_scene, "seq", axis=1, tiled=True),
        lax.all_gather(v_scene, "seq", axis=1, tiled=True),
    )
    attended, row_lse = attend(q_scene, k_gathered, v_gathered)
    att_low = attended.reshape(row_count, model_width).astype(jnp.bfloat16)
    residual = flat_rows + matmul(att_low, w_out) + b_out
    normed_two, norm_two_pull = jax.vjp(norm_rows, residual, gain_two, shift_two)
    normed_two_low = normed_two.astype(jnp.bfloat16)
    hidden = matmul(normed_two_low, w_up) + b_up
    activated, gelu_pull = jax.vjp(gelu_tanh, hidden)
    act_low = activated.astype(jnp.bfloat16)
    block_rows = residual + matmul(act_low, w_down) + b_down
    block_out = block_rows.reshape(scenes, local_len, model_width).astype(jnp.bfloat16)
    masked_f = out_grad.astype(jnp.float32) * surface_mask.astype(jnp.float32)[..., None]
    masked_rows = masked_f.reshape(row_count, model_width)
    masked_low = masked_rows.astype(jnp.bfloat16)
    grad_down = matmul_tn(act_low, masked_low)
    grad_bdown = jnp.sum(masked_rows, axis=0)
    act_grad = matmul_nt(masked_low, w_down)
    hidden_low = gelu_pull(act_grad)[0].astype(jnp.bfloat16)
    grad_up = matmul_tn(normed_two_low, hidden_low)
    grad_bup = jnp.sum(hidden_low.astype(jnp.float32), axis=0)
    norm_two_in = matmul_nt(hidden_low, w_up)
    resid_part, grad_gain_two, grad_shift_two = norm_two_pull(norm_two_in)
    resid_grad = masked_rows + resid_part
    resid_low = resid_grad.astype(jnp.bfloat16)
    grad_out = matmul_tn(att_low, resid_low)
    grad_bout = jnp.sum(resid_low.astype(jnp.float32), axis=0)
    att_grad = (
        matmul_nt(resid_low, w_out).astype(jnp.bfloat16).reshape(scenes, local_len, model_width)
    )
    q_parts, delta_parts, k_parts, v_parts = query_side(
        q_scene, k_gathered, v_gathered, row_lse, att_grad
    )
    k_summed, v_summed = (
        lax.psum_scatter(
            k_parts.astype(jnp.bfloat16), "seq", scatter_dimension=2, tiled=True
        ).astype(jnp.float32),
        lax.psum_scatter(
            v_parts.astype(jnp.bfloat16), "seq", scatter_dimension=2, tiled=True
        ).astype(jnp.float32),
    )
    k_grad = join_pairs(k_summed)
    v_grad = join_pairs(v_summed)
    q_grad = join_pairs(q_parts)
    q_grad_low = q_grad.reshape(row_count, model_width).astype(jnp.bfloat16)
    k_grad_low = k_grad.reshape(row_count, model_width).astype(jnp.bfloat16)
    v_grad_low = v_grad.reshape(row_count, model_width).astype(jnp.bfloat16)
    grad_query = matmul_tn(normed_low, q_grad_low)
    grad_key = matmul_tn(normed_low, k_grad_low)
    grad_value = matmul_tn(normed_low, v_grad_low)
    grad_bquery = jnp.sum(q_grad_low.astype(jnp.float32), axis=0)
    grad_bvalue = jnp.sum(v_grad_low.astype(jnp.float32), axis=0)
    norm_one_in = (
        matmul_nt(q_grad_low, w_query)
        + matmul_nt(k_grad_low, w_key)
        + matmul_nt(v_grad_low, w_value)
    )
    token_part, grad_gain_one, grad_shift_one = norm_one_pull(norm_one_in)
    tokens_grad = (
        (resid_grad + token_part).reshape(scenes, local_len, model_width).astype(jnp.bfloat16)
    )
    (
        sum_query,
        sum_key,
        sum_value,
        sum_out,
        sum_bquery,
        sum_bvalue,
        sum_bout,
        sum_gain_one,
        sum_shift_one,
        sum_up,
        sum_down,
        sum_bup,
        sum_bdown,
        sum_gain_two,
        sum_shift_two,
    ) = (
        lax.psum_scatter(grad_query, ("scene", "seq"), scatter_dimension=0, tiled=True),
        lax.psum_scatter(grad_key, ("scene", "seq"), scatter_dimension=0, tiled=True),
        lax.psum_scatter(grad_value, ("scene", "seq"), scatter_dimension=0, tiled=True),
        lax.psum_scatter(grad_out, ("scene", "seq"), scatter_dimension=0, tiled=True),
        lax.psum_scatter(grad_bquery, ("scene", "seq"), scatter_dimension=0, tiled=True),
        lax.psum_scatter(grad_bvalue, ("scene", "seq"), scatter_dimension=0, tiled=True),
        lax.psum_scatter(grad_bout, ("scene", "seq"), scatter_dimension=0, tiled=True),
        lax.psum_scatter(grad_gain_one, ("scene", "seq"), scatter_dimension=0, tiled=True),
        lax.psum_scatter(grad_shift_one, ("scene", "seq"), scatter_dimension=0, tiled=True),
        lax.psum_scatter(grad_up, ("scene", "seq"), scatter_dimension=0, tiled=True),
        lax.psum_scatter(grad_down, ("scene", "seq"), scatter_dimension=0, tiled=True),
        lax.psum_scatter(grad_bup, ("scene", "seq"), scatter_dimension=0, tiled=True),
        lax.psum_scatter(grad_bdown, ("scene", "seq"), scatter_dimension=0, tiled=True),
        lax.psum_scatter(grad_gain_two, ("scene", "seq"), scatter_dimension=0, tiled=True),
        lax.psum_scatter(grad_shift_two, ("scene", "seq"), scatter_dimension=0, tiled=True),
    )
    return (
        block_out,
        tokens_grad,
        sum_query,
        sum_key,
        sum_value,
        sum_out,
        sum_up,
        sum_down,
        sum_bquery,
        sum_bvalue,
        sum_bout,
        sum_bup,
        sum_bdown,
        sum_gain_one,
        sum_shift_one,
        sum_gain_two,
        sum_shift_two,
    )


def solution(mesh):
    placed = (
        P("scene", "seq", None),
        P("scene", "seq"),
        P("scene", "seq", None),
        P(),
        P(),
        P(),
        P(),
        P(),
        P(),
        P(),
        P(),
        P(),
        P(),
        P(),
        P(),
        P(),
        P(),
        P(),
    )
    return jax.shard_map(
        on_device,
        mesh=mesh,
        in_specs=placed,
        out_specs=(
            P("scene", "seq", None),
            P("scene", "seq", None),
            P(("scene", "seq"), None),
            P(("scene", "seq"), None),
            P(("scene", "seq"), None),
            P(("scene", "seq"), None),
            P(("scene", "seq"), None),
            P(("scene", "seq"), None),
            P(("scene", "seq")),
            P(("scene", "seq")),
            P(("scene", "seq")),
            P(("scene", "seq")),
            P(("scene", "seq")),
            P(("scene", "seq")),
            P(("scene", "seq")),
            P(("scene", "seq")),
            P(("scene", "seq")),
        ),
        check_vma=False,
    )
```

profile of v0, /device:TPU:0, one launch (start us, length us, event | category | flops | bytes accessed | tf_op | source)
XLA Modules:
  0.0 1662.1 jit_solution(7076041561755759142)
XLA Ops:
  18.6 72.6 %all-gather.7.cloned.1.call-done = bf16[4096,1024]{1,0:T(8,128)(2,1)} async-done(((bf16[256,1024]{1,0:T(8,128)(2,1)}), bf16[4096,1024]{1,0:T(8,128)(2,1)}) %all-gather.7.cloned.1.call-update) | async-done | bytes 8388624 | tf_op jit(solution)/shard_map/all_gather | solution.py:164
  91.2 11.3 copy.44
  102.5 64.6 %all-gather.5.cloned.1.call-done = bf16[4096,1024]{1,0:T(8,128)(2,1)} async-done(((bf16[256,1024]{1,0:T(8,128)(2,1)}), bf16[4096,1024]{1,0:T(8,128)(2,1)}) %all-gather.5.cloned.1.call-update) | async-done | bytes 8388624 | tf_op jit(solution)/shard_map/all_gather | solution.py:165
  167.1 11.3 copy.42
  178.5 71.2 %while.26 = (s32[]{:T(128)}, bf16[8,1,256,128]{2,3,1,0:T(8,128)(2,1)S(1)}, f32[8,1,2,256]{3,2,1,0:T(2,128)S(1)}, s32[8]{0:T(128)S(1)}, bf16[1,4096,1024]{1,2,0:T...) while((s32[]{:T(128)}, ...), condition=%wide.region_5.6_spmd, body=%wide.region_2.5_spmd.sunk | while | flops 555744768 | bytes 31867072 | solution.py:89
  252.8 6.0 convolution_add_fusion
  258.8 6.5 convert_reduce_fusion
  273.2 234.4 %while.27 = (s32[]{:T(128)}, bf16[8,1,256,128]{2,3,1,0:T(8,128)(2,1)}, bf16[8,1,4096,128]{2,3,1,0:T(8,128)(2,1)}, bf16[8,1,4096,128]{2,3,1,0:T(8,128)(2,1)}, s32...) while((s32[]{:T(128)}, ...), condition=%wide.region_12.13_spmd, body=%wide.region_10.12_spmd.sunk | while | flops 1360068096 | bytes 123546016 | solution.py:126
  280.1 4.9 multiply_reduce_fusion.8
  285.8 7.9 multiply_convert_fusion.5
  315.1 7.9 multiply_convert_fusion.5
  344.4 7.9 multiply_convert_fusion.5
  373.7 7.9 multiply_convert_fusion.5
  397.3 4.9 multiply_reduce_fusion.8
  403.0 7.9 multiply_convert_fusion.5
  432.3 7.9 multiply_convert_fusion.5
  455.9 4.9 multiply_reduce_fusion.8
  461.6 7.9 multiply_convert_fusion.5
  490.9 7.9 multiply_convert_fusion.5
  511.6 11.2 reduce-scatter.13.cloned.1.call-start
  525.8 85.0 %reduce-scatter.11.cloned.1.call-done = bf16[8,1,256,128]{2,3,1,0:T(8,128)(2,1)} async-done(((bf16[8,1,4096,128]{2,3,1,0:T(8,128)(2,1)}), bf16[8,1,256,128]{2,3,1,0:T(8,128)(2,1)}) %reduce-scatter.11.cloned.1.call-update) | async-done | bytes 524304 | tf_op jit(solution)/shard_map/reduce_scatter | solution.py:202
  614.8 104.6 %reduce-scatter.9.cloned.1.call-done = bf16[8,1,256,128]{2,3,1,0:T(8,128)(2,1)} async-done(((bf16[8,1,4096,128]{2,3,1,0:T(8,128)(2,1)}), bf16[8,1,256,128]{2,3,1,0:T(8,128)(2,1)}) %reduce-scatter.9.cloned.1.call-update) | async-done | bytes 524304 | tf_op jit(solution)/shard_map/reduce_scatter | solution.py:199
  723.4 10.8 fusion.39
  734.9 10.2 fusion.44
  749.3 8.4 fusion.23
  761.3 41.4 %all-reduce.9 = (f32[1024]{0:T(1024)S(1)}, f32[1024]{0:T(1024)S(1)}, f32[1024]{0:T(1024)S(1)}, f32[4096]{0:T(1024)S(1)}, f32[1024]{0:T(1024)S(1)}, /*index=5*/f3...) all-reduce(f32[1024]{0:T(1024)S(1)} %bitcast.240, ...), channel_id=12, replica_groups=mesh['scene'=2,'seq'=16] {'scene','seq'}, use_global_device_ids=true, to_apply=%region_24.25.clone | all-reduce | flops 12288 | bytes 98304
  810.8 52.2 %reduce-scatter.19.cloned.1.call-done = f32[32,1024]{1,0:T(8,128)} async-done(((f32[1024,1024]{1,0:T(8,128)}), f32[32,1024]{1,0:T(8,128)}) %reduce-scatter.19.cloned.1.call-update) | async-done | bytes 131088 | tf_op jit(solution)/shard_map/reduce_scatter | solution.py:246
  863.0 140.4 %reduce-scatter.13.cloned.1.call-done = f32[32,1024]{1,0:T(8,128)} async-done(((f32[1024,1024]{1,0:T(8,128)}), f32[32,1024]{1,0:T(8,128)}) %reduce-scatter.13.cloned.1.call-update) | async-done | bytes 131088 | tf_op jit(solution)/shard_map/reduce_scatter | solution.py:243
  1003.4 140.7 %reduce-scatter.17.cloned.1.call-done = f32[32,1024]{1,0:T(8,128)} async-done(((f32[1024,1024]{1,0:T(8,128)}), f32[32,1024]{1,0:T(8,128)}) %reduce-scatter.17.cloned.1.call-update) | async-done | bytes 131088 | tf_op jit(solution)/shard_map/reduce_scatter | solution.py:245
  1144.2 140.1 %reduce-scatter.15.cloned.1.call-done = f32[32,1024]{1,0:T(8,128)} async-done(((f32[1024,1024]{1,0:T(8,128)}), f32[32,1024]{1,0:T(8,128)}) %reduce-scatter.15.cloned.1.call-update) | async-done | bytes 131088 | tf_op jit(solution)/shard_map/reduce_scatter | solution.py:244
  1284.3 183.5 %reduce-scatter.23.cloned.1.call-done = f32[128,1024]{1,0:T(8,128)} async-done(((f32[4096,1024]{1,0:T(8,128)}), f32[128,1024]{1,0:T(8,128)}) %reduce-scatter.23.cloned.1.call-update) | async-done | bytes 524304 | tf_op jit(solution)/shard_map/reduce_scatter | solution.py:253
  1467.8 187.3 %reduce-scatter.21.cloned.1.call-done = f32[32,4096]{1,0:T(8,128)} async-done(((f32[1024,4096]{1,0:T(8,128)}), f32[32,4096]{1,0:T(8,128)}) %reduce-scatter.21.cloned.1.call-update) | async-done | bytes 524304 | tf_op jit(solution)/shard_map/reduce_scatter | solution.py:252
  (422 shorter events, 263.7 us)
Async XLA Ops:
  7.2 83.9 %all-gather.7.cloned.1.call-start = ((), (), s32[]{:S(2)}) async-start(), calls=%async_computation.17 | async-start | bytes 8912896 | tf_op jit(solution)/shard_map/all_gather | solution.py:164
  13.4 153.7 %all-gather.5.cloned.1.call-start = ((), (), s32[]{:S(2)}) async-start(), calls=%async_computation.16 | async-start | bytes 8912896 | tf_op jit(solution)/shard_map/all_gather | solution.py:165
  15.1 595.7 %reduce-scatter.11.cloned.1.call-start = ((), (), s32[]{:S(2)}) async-start(), calls=%async_computation.9 | async-start | bytes 8912896 | tf_op jit(solution)/shard_map/reduce_scatter | solution.py:202
  178.5 71.3 %copy-start.36 = (f32[1024]{0:T(1024)S(1)}, f32[1024]{0:T(1024)}, u32[]{:S(2)}) copy-start(f32[1024]{0:T(1024)} %param.33) | copy-start | bytes 12292
  249.7 9.0 copy-start.13
  249.8 9.0 slice-start.2
  252.4 16.1 copy-start.6
  252.8 12.6 slice-start
  273.2 6.9 copy-start.23
  302.5 6.9 copy-start.23
  331.8 6.9 copy-start.23
  361.0 6.9 copy-start.23
  390.3 6.9 copy-start.23
  419.6 6.9 copy-start.23
  449.0 6.9 copy-start.23
  507.6 211.8 %reduce-scatter.9.cloned.1.call-start = ((), (), s32[]{:S(2)}) async-start(), calls=%async_computation.8 | async-start | bytes 8912896 | tf_op jit(solution)/shard_map/reduce_scatter | solution.py:199
  508.2 354.8 %reduce-scatter.19.cloned.1.call-start = ((), (), s32[]{:S(2)}) async-start(), calls=%async_computation.13 | async-start | bytes 4325376 | tf_op jit(solution)/shard_map/reduce_scatter | solution.py:246
  511.5 11.2 copy-start.5
  511.5 11.2 copy-start.12
  511.5 11.2 copy-start.27
  511.5 11.2 copy-start.31
  511.5 11.3 copy-start.33
  511.5 11.2 copy-start.35
  511.6 491.8 %reduce-scatter.13.cloned.1.call-start = ((), (), s32[]{:S(2)}) async-start(), calls=%async_computation.10 | async-start | bytes 4325376 | tf_op jit(solution)/shard_map/reduce_scatter | solution.py:243
  525.8 618.4 %reduce-scatter.17.cloned.1.call-start = ((), (), s32[]{:S(2)}) async-start(), calls=%async_computation.12 | async-start | bytes 4325376 | tf_op jit(solution)/shard_map/reduce_scatter | solution.py:245
  614.7 669.6 %reduce-scatter.15.cloned.1.call-start = ((), (), s32[]{:S(2)}) async-start(), calls=%async_computation.11 | async-start | bytes 4325376 | tf_op jit(solution)/shard_map/reduce_scatter | solution.py:244
  723.3 744.4 %reduce-scatter.23.cloned.1.call-start = ((), (), s32[]{:S(2)}) async-start(), calls=%async_computation.15 | async-start | bytes 17301504 | tf_op jit(solution)/shard_map/reduce_scatter | solution.py:253
  734.3 920.8 %reduce-scatter.21.cloned.1.call-start = ((), (), s32[]{:S(2)}) async-start(), calls=%async_computation.14 | async-start | bytes 17301504 | tf_op jit(solution)/shard_map/reduce_scatter | solution.py:252
  749.3 8.4 copy-start.16
  749.3 8.6 copy-start.19
  749.3 8.6 copy-start.21
  758.7 49.2 %copy-start.40 = (f32[256]{0:T(256)S(1)}, f32[256]{0:T(256)}, u32[]{:S(2)}) copy-start(f32[256]{0:T(256)} %copy-done.39) | copy-start | bytes 3076
  (67 other events, 245.5 us)
Sparse Core Ops, SparseCore 0:
  13.5 77.5 all-gather.6
  93.9 73.1 all-gather.4
  507.7 103.0 reduce-scatter.10
  614.8 104.5 reduce-scatter.8
  722.1 140.8 reduce-scatter.18
  865.7 137.6 reduce-scatter.12
  1006.3 137.8 reduce-scatter.16
  1147.0 137.2 reduce-scatter.14
  1287.2 180.5 reduce-scatter.22
  1470.5 184.5 reduce-scatter.20
where the time goes:
time: 1670 us; the launch traced here: 1660 us
  waiting for transfers between devices  1170 us (70%)
  matrix products  203 us (12%)
  local copies, waits for them, and re-layouts  117 us (7%)
  other arithmetic  85 us (5%)
  blocking collectives  41.4 us (2%)
  loops' own time  17 us (1%)
    reduce_scatter x1, waiting for transfers between devices, on_device(): lax.psum_scatter(grad_up, ('scene', 'seq'), scatter_dimension=0, tiled=True)  187 us
    reduce_scatter x1, waiting for transfers between devices, on_device(): lax.psum_scatter(grad_down, ('scene', 'seq'), scatter_dimension=0, tiled=...  183 us
    reduce_scatter x1, waiting for transfers between devices, on_device(): lax.psum_scatter(grad_value, ('scene', 'seq'), scatter_dimension=0, tiled...  141 us
    reduce_scatter x1, waiting for transfers between devices, on_device(): lax.psum_scatter(grad_query, ('scene', 'seq'), scatter_dimension=0, tiled...  140 us
    reduce_scatter x1, waiting for transfers between devices, on_device(): lax.psum_scatter(grad_key, ('scene', 'seq'), scatter_dimension=0, tiled=T...  140 us
    reduce_scatter x1, waiting for transfers between devices, on_device(): lax.psum_scatter(k_parts.astype(jnp.bfloat16), 'seq', scatter_dimension=2...  105 us
    reduce_scatter x1, waiting for transfers between devices, on_device(): lax.psum_scatter(v_parts.astype(jnp.bfloat16), 'seq', scatter_dimension=2...  85 us
    all_gather x1, waiting for transfers between devices, on_device(): lax.all_gather(k_scene, 'seq', axis=1, tiled=True)  72.6 us
  transfers between devices with their start and end apart: 10, of which 10 were waited for; matrix products, arithmetic and copies ran while one was open for 4% of the time, Pallas kernels for 0%

commit v1 on v0

--- a/solution.py
+++ b/solution.py
@@ -1,15 +1,785 @@
+import functools
+
 import jax
 import jax.numpy as jnp
 from jax import lax
+from jax.experimental import pallas as pl
+from jax.experimental.pallas import tpu as pltpu
 from jax.sharding import PartitionSpec as P
 
 HEADS = 16
 HEAD_DIM = 64
-
+MESH = pl.DeviceIdType.MESH
+f32 = jnp.float32
+bf16 = jnp.bfloat16
 
 norm_eps = 1e-05
 score_scale = 0.125
 gelu_coef = 0.7978845608028654
+
+
+def matmul(left, right):
+    return jnp.dot(left, right, preferred_element_type=jnp.float32)
+
+
+def contract(left, right, left_dim, right_dim):
+    return lax.dot_general(
+        left, right, (((left_dim,), (right_dim,)), ((), ())), preferred_element_type=jnp.float32
+    )
+
+
+def matmul_tn(left, right):
+    return contract(left, right, 0, 0)
+
+
+def matmul_nt(left, right):
+    return contract(left, right, 1, 1)
+
+
+def greet(partners):
+    barrier = pltpu.get_barrier_semaphore()
+    for partner in partners:
+        pl.semaphore_signal(barrier, inc=1, device_id=partner, device_id_type=MESH)
+    pl.semaphore_wait(barrier, len(partners))
+
+
+def remote(src, dst, send_sem, recv_sem, device):
+    return pltpu.make_async_remote_copy(
+        src_ref=src,
+        dst_ref=dst,
+        send_sem=send_sem,
+        recv_sem=recv_sem,
+        device_id=device,
+        device_id_type=MESH,
+    )
+
+
+def forward_kernel(
+    n,
+    tok,
+    qt_ref,
+    kt_ref,
+    vt_ref,
+    att_ref,
+    q_out,
+    k_out,
+    v_out,
+    o_out,
+    lse_out,
+    q_all,
+    k_all,
+    v_all,
+    k_nat,
+    o_all,
+    lse_all,
+    att_send,
+    in_send,
+    in_recv,
+    in_local,
+    out_send,
+    out_recv,
+    out_local,
+    save_sem,
+):
+    me = lax.axis_index("seq")
+    scene = lax.axis_index("scene")
+    chip, core = me // 2, lax.rem(me, 2)
+    chips = n // 2
+    length = n * tok
+    others = [lax.rem(me + j, n) for j in range(1, n)]
+    greet([(scene, other) for other in others])
+
+    def rows(head):
+        return pl.ds(pl.multiple_of(head * HEAD_DIM, HEAD_DIM), HEAD_DIM)
+
+    def lanes(block, width=tok):
+        return pl.ds(pl.multiple_of(block * width, width), width)
+
+    pairs = ((kt_ref, k_all), (vt_ref, v_all), (qt_ref, q_all))
+    copies = {}
+    for a, (src, dst) in enumerate(pairs):
+        for j in range(1, n):
+            head = lax.rem(me + j, n)
+            copies[a, j] = remote(
+                src.at[rows(head), :],
+                dst.at[:, lanes(me)],
+                in_send.at[a, j],
+                in_recv.at[a, j],
+                (scene, head),
+            )
+            copies[a, j].start()
+    local = [
+        pltpu.make_async_copy(src.at[rows(me), :], dst.at[:, lanes(me)], in_local.at[a])
+        for a, (src, dst) in enumerate(pairs)
+    ]
+    for copy in local:
+        copy.start()
+    for copy in local:
+        copy.wait()
+    for a in range(3):
+        for j in range(1, n):
+            copies[a, j].wait_recv()
+    k_nat[...] = k_all[...].T
+    saves = [
+        pltpu.make_async_copy(src, dst, save_sem.at[a])
+        for a, (src, dst) in enumerate(((q_all, q_out), (k_all, k_out), (v_all, v_out)))
+    ]
+    for copy in saves:
+        copy.start()
+
+    wide = 2 * tok
+    key_block = length // 2
+
+    def queries(step):
+        target = lax.rem(chip + step, chips)
+        span = lanes(target, wide)
+        q_here = q_all[:, span]
+        top = total = acc = None
+        for block in range(length // key_block):
+            keys = slice(block * key_block, (block + 1) * key_block)
+            scores = contract(k_nat[keys, :], q_here, 1, 0)
+            here = jnp.max(scores, axis=0, keepdims=True)
+            new_top = here if top is None else jnp.maximum(top, here)
+            shifted = jnp.exp(scores - new_top)
+            part_sum = jnp.sum(shifted, axis=0, keepdims=True)
+            part = contract(v_all[:, keys], shifted.astype(bf16), 1, 0)
+            if top is None:
+                total, acc = part_sum, part
+            else:
+                fade = jnp.exp(top - new_top)
+                total, acc = total * fade + part_sum, acc * fade + part
+            top = new_top
+        out = acc / total
+        o_all[:, span] = out
+        lse_all[:, span] = jnp.broadcast_to(top + jnp.log(total), (8, wide))
+        low = out.astype(bf16)
+        att_send[step, 0] = low[:, :tok]
+        att_send[step, 1] = low[:, tok:]
+        return target
+
+    def out_copy(step, target, flip):
+        device = 2 * target + lax.rem(core + flip, 2)
+        return remote(
+            att_send.at[step, lax.rem(core + flip, 2)],
+            att_ref.at[rows(me), :],
+            out_send.at[step, flip],
+            out_recv.at[step, flip],
+            (scene, device),
+        )
+
+    queries(0)
+    mine = pltpu.make_async_copy(att_send.at[0, core], att_ref.at[rows(me), :], out_local)
+    mine.start()
+    out_copy(0, chip, 1).start()
+
+    def step_body(step, carry):
+        target = queries(step)
+        out_copy(step, target, 0).start()
+        out_copy(step, target, 1).start()
+        return carry
+
+    lax.fori_loop(1, chips, step_body, 0)
+    o_save = pltpu.make_async_copy(o_all, o_out, save_sem.at[3])
+    l_save = pltpu.make_async_copy(lse_all, lse_out, save_sem.at[4])
+    o_save.start()
+    l_save.start()
+    for a in range(3):
+        for j in range(1, n):
+            copies[a, j].wait_send()
+    mine.wait()
+    out_copy(0, chip, 1).wait()
+
+    def drain(step, carry):
+        target = lax.rem(chip + step, chips)
+        out_copy(step, target, 0).wait()
+        out_copy(step, target, 1).wait()
+        return carry
+
+    lax.fori_loop(1, chips, drain, 0)
+    for copy in saves + [o_save, l_save]:
+        copy.wait()
+
+
+def attention_forward(n, q_t, k_t, v_t):
+    tok = q_t.shape[1]
+    length = n * tok
+    any_spec = pl.BlockSpec(memory_space=pl.ANY)
+    head_all = jax.ShapeDtypeStruct((HEAD_DIM, length), bf16)
+    dma = pltpu.SemaphoreType.DMA
+    return pl.pallas_call(
+        functools.partial(forward_kernel, n, tok),
+        out_shape=(
+            jax.ShapeDtypeStruct(q_t.shape, bf16),
+            head_all,
+            head_all,
+            head_all,
+            jax.ShapeDtypeStruct((HEAD_DIM, length), f32),
+            jax.ShapeDtypeStruct((8, length), f32),
+        ),
+        in_specs=[any_spec] * 3,
+        out_specs=[any_spec] * 6,
+        scratch_shapes=[
+            pltpu.VMEM((HEAD_DIM, length), bf16),
+            pltpu.VMEM((HEAD_DIM, length), bf16),
+            pltpu.VMEM((HEAD_DIM, length), bf16),
+            pltpu.VMEM((length, HEAD_DIM), bf16),
+            pltpu.VMEM((HEAD_DIM, length), f32),
+            pltpu.VMEM((8, length), f32),
+            pltpu.VMEM((n // 2, 2, HEAD_DIM, tok), bf16),
+            dma((3, n)),
+            dma((3, n)),
+            dma((3,)),
+            dma((n // 2, 2)),
+            dma((n // 2, 2)),
+            dma,
+            dma((5,)),
+        ],
+        compiler_params=pltpu.CompilerParams(
+            collective_id=0, has_side_effects=True, vmem_limit_bytes=48 << 20
+        ),
+        name="attention_forward",
+    )(q_t, k_t, v_t)
+
+
+def backward_kernel(
+    n,
+    tok,
+    dt_ref,
+    q_all,
+    k_all,
+    v_all,
+    o_all,
+    lse_all,
+    dq_ref,
+    dk_ref,
+    dv_ref,
+    heads_ref,
+    d_all,
+    q_nat,
+    k_nat,
+    v_nat,
+    d_nat,
+    delta,
+    dq_acc,
+    low,
+    in_send,
+    in_recv,
+    in_local,
+    kv_send,
+    kv_recv,
+    kv_local,
+    q_send,
+    q_recv,
+    q_local,
+    save_sem,
+):
+    me = lax.axis_index("seq")
+    scene = lax.axis_index("scene")
+    chip, core = me // 2, lax.rem(me, 2)
+    chips = n // 2
+    length = n * tok
+    wide = 2 * tok
+    greet([(scene, lax.rem(me + j, n)) for j in range(1, n)])
+
+    def rows(head):
+        return pl.ds(pl.multiple_of(head * HEAD_DIM, HEAD_DIM), HEAD_DIM)
+
+    def lanes(block, width=tok):
+        return pl.ds(pl.multiple_of(block * width, width), width)
+
+    copies = []
+    for j in range(1, n):
+        head = lax.rem(me + j, n)
+        copies.append(
+            remote(
+                dt_ref.at[rows(head), :],
+                d_all.at[:, lanes(me)],
+                in_send.at[j],
+                in_recv.at[j],
+                (scene, head),
+            )
+        )
+        copies[-1].start()
+    local = pltpu.make_async_copy(dt_ref.at[rows(me), :], d_all.at[:, lanes(me)], in_local)
+    local.start()
+    q_nat[...] = q_all[...].T
+    k_nat[...] = k_all[...].T
+    v_nat[...] = v_all[...].T
+    dq_acc[...] = jnp.zeros_like(dq_acc)
+    local.wait()
+    for copy in copies:
+        copy.wait_recv()
+    d_nat[...] = d_all[...].T
+    delta[...] = jnp.broadcast_to(
+        jnp.sum(d_all[...].astype(f32) * o_all[...], axis=0, keepdims=True), delta.shape
+    )
+
+    def q_copy(step, flip):
+        target = lax.rem(chip + step, chips)
+        device = 2 * target + lax.rem(core + flip, 2)
+        return remote(
+            low.at[0, :, lanes(device)],
+            dq_ref.at[rows(me), :],
+            q_send.at[step, flip],
+            q_recv.at[step, flip],
+            (scene, device),
+        )
+
+    def kv_copy(a, step, flip):
+        target = lax.rem(chip + step, chips)
+        device = 2 * target + lax.rem(core + flip, 2)
+        return remote(
+            low.at[1 + a, :, lanes(device)],
+            (dk_ref, dv_ref)[a].at[rows(me), :],
+            kv_send.at[a, step, flip],
+            kv_recv.at[a, step, flip],
+            (scene, device),
+        )
+
+    mine = [
+        pltpu.make_async_copy(low.at[0, :, lanes(me)], dq_ref.at[rows(me), :], q_local),
+        pltpu.make_async_copy(low.at[1, :, lanes(me)], dk_ref.at[rows(me), :], kv_local.at[0]),
+        pltpu.make_async_copy(low.at[2, :, lanes(me)], dv_ref.at[rows(me), :], kv_local.at[1]),
+    ]
+
+    def keys(step, last):
+        target = lax.rem(chip + step, chips)
+        span = lanes(target, wide)
+        k_here, v_here, kt_here = k_nat[span, :], v_nat[span, :], k_all[:, span]
+        dk = dv = None
+        for i in range(chips):
+            if last:
+                block = lax.rem(chip + i, chips)
+                there = lanes(block, wide)
+            else:
+                there = slice(i * wide, (i + 1) * wide)
+            scores = contract(k_here, q_all[:, there], 1, 0)
+            prob = jnp.exp(scores - lse_all[0:1, there])
+            dprob = contract(v_here, d_all[:, there], 1, 0)
+            dscore = (prob * (dprob - delta[0:1, there])).astype(bf16)
+            v_part = contract(prob.astype(bf16), d_nat[there, :], 1, 0)
+            k_part = contract(dscore, q_nat[there, :], 1, 0)
+            dk = k_part if dk is None else dk + k_part
+            dv = v_part if dv is None else dv + v_part
+            dq = dq_acc[:, there] + contract(kt_here, dscore, 1, 0)
+            if last:
+                low[0, :, there] = (dq * score_scale).astype(bf16)
+                if i == 0:
+                    mine[0].start()
+                else:
+                    q_copy(i, 0).start()
+                q_copy(i, 1).start()
+            else:
+                dq_acc[:, there] = dq
+        low[1, :, span] = dk.astype(bf16).T
+        low[2, :, span] = dv.astype(bf16).T
+
+    keys(0, False)
+    mine[1].start()
+    mine[2].start()
+    kv_copy(0, 0, 1).start()
+    kv_copy(1, 0, 1).start()
+
+    def send_kv(step):
+        for a in range(2):
+            kv_copy(a, step, 0).start()
+            kv_copy(a, step, 1).start()
+
+    def step_body(step, carry):
+        keys(step, False)
+        send_kv(step)
+        return carry
+
+    lax.fori_loop(1, chips - 1, step_body, 0)
+    keys(chips - 1, True)
+    send_kv(chips - 1)
+    save = pltpu.make_async_copy(low, heads_ref, save_sem)
+    save.start()
+    for copy in copies:
+        copy.wait_send()
+    for copy in mine:
+        copy.wait()
+    for step in range(chips):
+        for flip in range(2):
+            if step == 0 and flip == 0:
+                continue
+            kv_copy(0, step, flip).wait()
+            kv_copy(1, step, flip).wait()
+            q_copy(step, flip).wait()
+    save.wait()
+
+
+def attention_backward(n, d_t, q_all, k_all, v_all, o_all, lse_all):
+    tok = d_t.shape[1]
+    length = n * tok
+    chips = n // 2
+    any_spec = pl.BlockSpec(memory_space=pl.ANY)
+    vmem = pl.BlockSpec(memory_space=pltpu.VMEM)
+    dma = pltpu.SemaphoreType.DMA
+    part = jax.ShapeDtypeStruct(d_t.shape, bf16)
+    return pl.pallas_call(
+        functools.partial(backward_kernel, n, tok),
+        out_shape=(part, part, part, jax.ShapeDtypeStruct((3, HEAD_DIM, length), bf16)),
+        in_specs=[any_spec] + [vmem] * 5,
+        out_specs=[any_spec] * 4,
+        scratch_shapes=[
+            pltpu.VMEM((HEAD_DIM, length), bf16),
+            pltpu.VMEM((length, HEAD_DIM), bf16),
+            pltpu.VMEM((length, HEAD_DIM), bf16),
+            pltpu.VMEM((length, HEAD_DIM), bf16),
+            pltpu.VMEM((length, HEAD_DIM), bf16),
+            pltpu.VMEM((8, length), f32),
+            pltpu.VMEM((HEAD_DIM, length), f32),
+            pltpu.VMEM((3, HEAD_DIM, length), bf16),
+            dma((n,)),
+            dma((n,)),
+            dma,
+            dma((2, chips, 2)),
+            dma((2, chips, 2)),
+            dma((2,)),
+            dma((chips, 2)),
+            dma((chips, 2)),
+            dma,
+            dma,
+        ],
+        compiler_params=pltpu.CompilerParams(
+            collective_id=1, has_side_effects=True, vmem_limit_bytes=48 << 20
+        ),
+        name="attention_backward",
+    )(d_t, q_all, k_all, v_all, o_all, lse_all)
+
+
+def halving_kernel(
+    down_ref,
+    up_ref,
+    out_ref,
+    down_sum,
+    up_sum,
+    out_sum,
+    own,
+    got0,
+    got1a,
+    got1b,
+    got2,
+    got3,
+    got4,
+    load_sem,
+    send_sem,
+    recv_sem,
+):
+    me = lax.axis_index("seq")
+    x = lax.axis_index("scene")
+    core = lax.rem(me, 2)
+    y = lax.rem(me // 2, 2)
+    z0 = lax.rem(me // 4, 2)
+    z1 = me // 8
+    at_core = (x, me + 1 - 2 * core)
+    at_x = (1 - x, me)
+    at_y = (x, me + 2 - 4 * y)
+    at_z0 = (x, me + 4 - 8 * z0)
+    at_z1 = (x, me + 8 - 16 * z1)
+    greet([at_core, at_x, at_y, at_z0, at_z1])
+
+    every = slice(None)
+    pieces = (
+        [(down_ref, down_sum, slice(32 * i, 32 * i + 32), every) for i in range(4)]
+        + [(up_ref, up_sum, every, slice(1024 * i, 1024 * i + 1024)) for i in range(4)]
+        + [(out_ref, out_sum, every, every)]
+    )
+    top, low = slice(0, 16), slice(16, 32)
+    started = []
+    flight = {}
+
+    def send(src, dst, chunk, slot, device):
+        copy = remote(src, dst, send_sem.at[chunk, slot], recv_sem.at[chunk, slot], device)
+        copy.start()
+        started.append(copy)
+        return copy
+
+    for c, (ref, _, rows, columns) in enumerate(pieces):
+        load = pltpu.make_async_copy(
+            ref.at[:, :, :, core, rows, columns], own.at[c], load_sem.at[c]
+        )
+        load.start()
+        flight[c, 0] = (
+            load,
+            send(ref.at[:, :, :, 1 - core, rows, columns], got0.at[c], c, 0, at_core),
+        )
+
+    def stage1(c):
+        flight[c, 0][0].wait()
+        flight[c, 0][1].wait_recv()
+        own[c] = own[c] + got0[c]
+        flight[c, 1] = (
+            send(own.at[c, 1 - x, :, :, top, :], got1a.at[c], c, 1, at_x),
+            send(own.at[c, :, :, 1 - y, low, :], got1b.at[c], c, 2, at_y),
+        )
+
+    def stage2(c):
+        flight[c, 1][0].wait_recv()
+        got1a[c] = own[c, x, :, :, top, :] + got1a[c]
+        first = send(got1a.at[c, :, 1 - y], got2.at[c, :, top, :], c, 3, at_y)
+        flight[c, 1][1].wait_recv()
+        got1b[c] = own[c, :, :, y, low, :] + got1b[c]
+        flight[c, 2] = (first, send(got1b.at[c, 1 - x], got2.at[c, :, low, :], c, 4, at_x))
+
+    def stage3(c):
+        flight[c, 2][0].wait_recv()
+        got2[c, :, top, :] = got1a[c, :, y] + got2[c, :, top, :]
+        flight[c, 2][1].wait_recv()
+        got2[c, :, low, :] = got1b[c, x] + got2[c, :, low, :]
+        flight[c, 3] = (
+            send(got2.at[c, 1 - z0], got3.at[c, 0], c, 5, at_z0),
+            send(got2.at[c, 3 - z0], got3.at[c, 1], c, 6, at_z0),
+        )
+
+    def stage4(c):
+        flight[c, 3][0].wait_recv()
+        flight[c, 3][1].wait_recv()
+        got3[c, 0] = got2[c, z0] + got3[c, 0]
+        got3[c, 1] = got2[c, 2 + z0] + got3[c, 1]
+        flight[c, 4] = (send(got3.at[c, 1 - z1], got4.at[c], c, 7, at_z1),)
+
+    def stage5(c):
+        flight[c, 4][0].wait_recv()
+        _, ref, rows, columns = pieces[c]
+        ref[rows, columns] = got3[c, z1].astype(f32) + got4[c].astype(f32)
+
+    stages = (stage1, stage2, stage3, stage4, stage5)
+    for tick in range(len(pieces) + len(stages) - 1):
+        for depth in reversed(range(len(stages))):
+            if 0 <= tick - depth < len(pieces):
+                stages[depth](tick - depth)
+    for copy in started:
+        copy.wait_send()
+
+
+def halving_sum(down, up, out):
+    shards = 32
+    any_spec = pl.BlockSpec(memory_space=pl.ANY)
+    vmem = pl.BlockSpec(memory_space=pltpu.VMEM)
+    dma = pltpu.SemaphoreType.DMA
+    arrays = [down, up, out]
+    chunks = 9
+    return pl.pallas_call(
+        halving_kernel,
+        out_shape=tuple(
+            jax.ShapeDtypeStruct((a.shape[0] // shards, a.shape[1]), f32) for a in arrays
+        ),
+        in_specs=[any_spec] * 3,
+        out_specs=[vmem] * 3,
+        scratch_shapes=[
+            pltpu.VMEM((chunks, 2, 4, 2, 32, 1024), bf16),
+            pltpu.VMEM((chunks, 2, 4, 2, 32, 1024), bf16),
+            pltpu.VMEM((chunks, 4, 2, 16, 1024), bf16),
+            pltpu.VMEM((chunks, 2, 4, 16, 1024), bf16),
+            pltpu.VMEM((chunks, 4, 32, 1024), bf16),
+            pltpu.VMEM((chunks, 2, 32, 1024), bf16),
+            pltpu.VMEM((chunks, 32, 1024), bf16),
+            dma((chunks,)),
+            dma((chunks, 8)),
+            dma((chunks, 8)),
+        ],
+        compiler_params=pltpu.CompilerParams(
+            collective_id=2, has_side_effects=True, vmem_limit_bytes=48 << 20
+        ),
+        name="halving_sum",
+    )(*(a.reshape(2, 4, 2, 2, a.shape[0] // shards, a.shape[1]) for a in arrays))
+
+
+def exchange_kernel(scenes, n, count, *refs):
+    sources, sinks = refs[:count], refs[count : 2 * count]
+    send_sem, recv_sem, local_sem = refs[2 * count :]
+    me = lax.axis_index("seq")
+    scene = lax.axis_index("scene")
+    mine = scene * n + me
+    devices = scenes * n
+
+    def peer(j):
+        index = lax.rem(mine + j, devices)
+        return index, (index // n, lax.rem(index, n))
+
+    greet([peer(j)[1] for j in range(1, devices)])
+    copies = []
+    for a in range(count):
+        copies.append(
+            pltpu.make_async_copy(sources[a].at[mine], sinks[a].at[mine], local_sem.at[a])
+        )
+        copies[-1].start()
+    for j in range(1, devices):
+        index, device = peer(j)
+        for a in range(count):
+            copies.append(
+                remote(
+                    sources[a].at[index],
+                    sinks[a].at[mine],
+                    send_sem.at[a, j],
+                    recv_sem.at[a, j],
+                    device,
+                )
+            )
+            copies[-1].start()
+    for copy in copies:
+        copy.wait()
+
+
+def exchange(scenes, n, *arrays):
+    any_spec = pl.BlockSpec(memory_space=pl.ANY)
+    dma = pltpu.SemaphoreType.DMA
+    count, devices = len(arrays), scenes * n
+    return pl.pallas_call(
+        functools.partial(exchange_kernel, scenes, n, count),
+        out_shape=tuple(jax.ShapeDtypeStruct(a.shape, a.dtype) for a in arrays),
+        in_specs=[any_spec] * count,
+        out_specs=[any_spec] * count,
+        scratch_shapes=[dma((count, devices)), dma((count, devices)), dma((count,))],
+        compiler_params=pltpu.CompilerParams(collective_id=3, has_side_effects=True),
+        name="exchange",
+    )(*arrays)
+
+
+def normalise(values):
+    row_mean = jnp.mean(values, axis=-1, keepdims=True)
+    centred = values - row_mean
+    row_var = jnp.mean(centred * centred, axis=-1, keepdims=True)
+    inverse = lax.rsqrt(row_var + norm_eps)
+    return centred * inverse, inverse
+
+
+def norm_back(grad, scaled, inverse, gain):
+    weighted = grad * gain
+    back = inverse * (
+        weighted
+        - jnp.mean(weighted, axis=-1, keepdims=True)
+        - scaled * jnp.mean(weighted * scaled, axis=-1, keepdims=True)
+    )
+    return back, jnp.sum(grad * scaled, axis=0), jnp.sum(grad, axis=0)
+
+
+def gelu_both(values):
+    cubic = gelu_coef * (values + 0.044715 * values * values * values)
+    bend = jnp.tanh(cubic)
+    slope = gelu_coef * (1.0 + 3.0 * 0.044715 * values * values)
+    grad = 0.5 * (1.0 + bend) + 0.5 * values * (1.0 - bend * bend) * slope
+    return 0.5 * values * (1.0 + bend), grad
+
+
+def layer_on_device(
+    scenes,
+    n,
+    tokens,
+    surface_mask,
+    out_grad,
+    w_query,
+    w_key,
+    w_value,
+    w_out,
+    w_up,
+    w_down,
+    b_query,
+    b_value,
+    b_out,
+    b_up,
+    b_down,
+    gain_one,
+    shift_one,
+    gain_two,
+    shift_two,
+):
+    _, tok, width = tokens.shape
+    devices = scenes * n
+    rows = tokens[0].astype(f32)
+    scaled_one, inverse_one = normalise(rows)
+    normed = (scaled_one * gain_one + shift_one).astype(bf16)
+    normed_all = lax.all_gather(normed, "seq", axis=0, tiled=True)
+    q_t = contract(w_query, normed, 0, 1) + b_query[:, None]
+    q_t = (q_t.astype(bf16).astype(f32) * score_scale).astype(bf16)
+    k_t = contract(w_key, normed, 0, 1).astype(bf16)
+    v_t = (contract(w_value, normed, 0, 1) + b_value[:, None]).astype(bf16)
+    att_t, q_all, k_all, v_all, o_all, lse_all = attention_forward(n, q_t, k_t, v_t)
+
+    residual = rows + matmul_tn(att_t, w_out) + b_out
+    scaled_two, inverse_two = normalise(residual)
+    normed_two = (scaled_two * gain_two + shift_two).astype(bf16)
+    hidden = matmul(normed_two, w_up) + b_up
+    activated, gelu_grad = gelu_both(hidden)
+    activated = activated.astype(bf16)
+    block_out = (residual + matmul(activated, w_down) + b_down).astype(bf16)
+    masked = out_grad[0] * surface_mask[0].astype(bf16)[:, None]
+    grad_down = matmul_tn(activated, masked).astype(bf16)
+    grad_bdown = jnp.sum(masked.astype(f32), axis=0)
+    hidden_grad = (matmul_nt(masked, w_down) * gelu_grad).astype(bf16)
+    grad_up = matmul_tn(normed_two, hidden_grad).astype(bf16)
+    grad_bup = jnp.sum(hidden_grad.astype(f32), axis=0)
+    norm_two_in = matmul_nt(hidden_grad, w_up)
+    resid_part, grad_gain_two, grad_shift_two = norm_back(
+        norm_two_in, scaled_two, inverse_two, gain_two
+    )
+    resid_grad = masked.astype(f32) + resid_part
+    resid_low = resid_grad.astype(bf16)
+    grad_out = matmul(att_t, resid_low).astype(bf16)
+    grad_bout = jnp.sum(resid_low.astype(f32), axis=0)
+    att_grad_t = matmul_nt(w_out, resid_low).astype(bf16)
+
+    sum_down, sum_up, sum_out = halving_sum(grad_down, grad_up, grad_out)
+    dq_t, dk_t, dv_t, heads_t = attention_backward(
+        n, att_grad_t, q_all, k_all, v_all, o_all, lse_all
+    )
+
+    head_grads = matmul(heads_t.reshape(3 * HEAD_DIM, n * tok), normed_all)
+    head_grads = head_grads.T.reshape(devices, width // devices, 3 * HEAD_DIM)
+    norm_one_in = (
+        contract(dq_t, w_query, 0, 1) + contract(dk_t, w_key, 0, 1) + contract(dv_t, w_value, 0, 1)
+    )
+    token_part, grad_gain_one, grad_shift_one = norm_back(
+        norm_one_in, scaled_one, inverse_one, gain_one
+    )
+    tokens_grad = (resid_grad + token_part).astype(bf16)
+    grad_bquery = jnp.sum(dq_t.astype(f32), axis=1)
+    grad_bvalue = jnp.sum(dv_t.astype(f32), axis=1)
+    small = [
+        grad_bquery,
+        grad_bvalue,
+        grad_bout,
+        grad_bup,
+        grad_bdown,
+        grad_gain_one,
+        grad_shift_one,
+        grad_gain_two,
+        grad_shift_two,
+    ]
+    packed = jnp.concatenate([s.reshape(devices, -1) for s in small], axis=1)
+    room = -packed.shape[1] % 1024
+    packed = jnp.pad(packed, ((0, 0), (0, room))).reshape(devices, -1, 128)
+    heads_got, small_got = exchange(scenes, n, head_grads, packed)
+    heads_sum = heads_got.reshape(scenes, n, width // devices, 3, HEAD_DIM).sum(axis=0)
+    weights = [
+        jnp.moveaxis(heads_sum[:, :, i], 0, 1).reshape(width // devices, width) for i in range(3)
+    ]
+    vectors = small_got.reshape(devices, -1).sum(axis=0)
+    parts, at = [], 0
+    for s in small:
+        size = s.shape[0] // devices
+        parts.append(vectors[at : at + size])
+        at += size
+    bquery, bvalue, bout, bup, bdown, gone, sone, gtwo, stwo = parts
+    return (
+        block_out[None],
+        tokens_grad[None],
+        *weights,
+        sum_out,
+        sum_up,
+        sum_down,
+        bquery,
+        bvalue,
+        bout,
+        bup,
+        bdown,
+        gone,
+        sone,
+        gtwo,
+        stwo,
+    )
 
 
 def norm_rows(values, gain, shift):
@@ -22,22 +792,6 @@
 def gelu_tanh(values):
     return (
         0.5 * values * (1.0 + jnp.tanh(gelu_coef * (values + 0.044715 * values * values * values)))
-    )
-
-
-def matmul(left, right):
-    return jnp.dot(left, right, preferred_element_type=jnp.float32)
-
-
-def matmul_tn(left, right):
-    return lax.dot_general(
-        left, right, (((0,), (0,)), ((), ())), preferred_element_type=jnp.float32
-    )
-
-
-def matmul_nt(left, right):
-    return lax.dot_general(
-        left, right, (((1,), (1,)), ((), ())), preferred_element_type=jnp.float32
     )
 
 
@@ -129,7 +883,7 @@
     return results
 
 
-def on_device(
+def on_any_device(
     tokens,
     surface_mask,
     out_grad,
@@ -298,6 +1052,11 @@
         P(),
         P(),
     )
+    scenes, n = mesh.shape["scene"], mesh.shape["seq"]
+    if (scenes, n) == (2, HEADS):
+        on_device = functools.partial(layer_on_device, scenes, n)
+    else:
+        on_device = on_any_device
     return jax.shard_map(
         on_device,
         mesh=mesh,

time: 1670 us -> 425 us (0.25)
  waiting for transfers between devices: 1170 us -> 0.02 us
  Pallas kernels: 0 us -> 298 us
  matrix products: 203 us -> 60.5 us
  local copies, waits for them, and re-layouts: 117 us -> 33.5 us
  other arithmetic: 85 us -> 12.6 us
  blocking collectives: 41.4 us -> 0 us
  loops' own time: 17 us -> 0 us
    reduce_scatter x8 -> x0, waiting for transfers between devices: 1030 us -> none  [the longest x1 187 us: on_device(): lax.psum_scatter(grad_up, ('scene', 'seq'), scatter_dimension=0, tiled=True)]
    pallas_call x0 -> x4, Pallas kernels: none -> 298 us  [the longest x1 106 us: halving_sum(): pl.pallas_call(halving_kernel, out_shape=tuple((jax.ShapeDtypeStruct((a.s...]
    dot_general x68 -> x12, matrix products: 179 us -> 40.1 us  [contract(): lax.dot_general(left, right, (((left_dim,), (right_dim,)), ((), ())), pre...]
    all_gather x2 -> x1, waiting for transfers between devices: 137 us -> 0.01 us  [layer_on_device(): normed_all = lax.all_gather(normed, 'seq', axis=0, tiled=True)]
    convert_element_type x10 -> x2, other arithmetic: 66.3 us -> 2.15 us  [the longest x1 2.13 us: layer_on_device(): normed = (scaled_one * gain_one + shift_one).astype(bf16)]
    dynamic_slice x72 -> x0, local copies, waits for them, and re-layouts: 59.2 us -> none  [the longest x56 49.1 us: take_pair(): lax.dynamic_slice_in_dim(array_in, pair_index * pair_width, pair_width, 2)]
    unnamed x1 -> x0, blocking collectives: 41.4 us -> none
    while x83 -> x0, local copies, waits for them, and re-layouts: 30.5 us -> none  [the longest x3 23.6 us: attend(): lax.scan(attend_pair_step, jnp.zeros((), jnp.float32), jnp.arange(pair_co...]
  transfers between devices with their start and end apart: 10 -> 1, of which waited for: 10 -> 0; matrix products, arithmetic and copies ran while one was open for 4% -> 14% of each run, Pallas kernels for 0% -> 64%
where the time goes in v1:
time: 425 us; the launch traced here: 420 us
  Pallas kernels  298 us (70%)
  matrix products  60.5 us (14%)
  local copies, waits for them, and re-layouts  33.5 us (8%)
  between operations  15 us (4%)
  other arithmetic  12.6 us (3%)
    pallas_call x1, Pallas kernels, halving_sum(): pl.pallas_call(halving_kernel, out_shape=tuple((jax.ShapeDtypeStruct((a.s...  106 us
    pallas_call x1, Pallas kernels, attention_forward(): pl.pallas_call(functools.partial(forward_kernel, n, tok), out_shape=(jax....  86 us
    pallas_call x1, Pallas kernels, attention_backward(): pl.pallas_call(functools.partial(backward_kernel, n, tok), out_shape=(par...  78 us
    dot_general x12, matrix products, contract(): lax.dot_general(left, right, (((left_dim,), (right_dim,)), ((), ())), pre...  40.1 us
    pallas_call x1, Pallas kernels, exchange(): pl.pallas_call(functools.partial(exchange_kernel, scenes, n, count), out_...  28.3 us
    dot_general x4, matrix products, matmul(): return jnp.dot(left, right, preferred_element_type=jnp.float32)  20.4 us
    dot_general x1, local copies, waits for them, and re-layouts, matmul(): return jnp.dot(left, right, preferred_element_type=jnp.float32)  11.6 us
  transfers between devices with their start and end apart: 1, of which 0 were waited for; matrix products, arithmetic and copies ran while one was open for 14% of the time, Pallas kernels for 64%

profile of v1, /device:TPU:0, one launch (start us, length us, event | category | flops | bytes accessed | tf_op | source)
XLA Modules:
  0.0 419.5 jit_solution(116726534272387872)
XLA Ops:
  7.3 1.3 convert_reduce_fusion.2
  8.6 1.3 fusion.35
  9.9 2.1 fusion.28
  12.1 2.8 fusion.23.kt_ref
  15.0 2.2 fusion.22.vt_ref
  18.3 86.0 %attention_forward.1 = (bf16[1024,256]{1,0:T(8,128)(2,1)S(1)}, bf16[64,4096]{1,0:T(8,128)(2,1)S(1)}, bf16[64,4096]{1,0:T(8,128)(2,1)S(1)}, bf16[64,4096]{1,0:T(8...) custom-call(bf16[1024,256]{1,0:T(8,128)(2,1)S(1)} %fusion.25.qt_ref, bf16[1024,256]{1,0:T(8,128)(2,1)S(1)} %fusion.23.kt_ref, ...), custom_call_target="tpu_custom_call" | custom-call | tf_op jit(solution)/shard_map/attention_forward/pallas_call | solution.py:209
  105.6 6.1 %convolution_add_fusion = f32[256,4096]{1,0:T(8,128)S(1)} fusion(bf16[1024,4096]{1,0:T(8,128)(2,1)} %param.25, f32[4096]{0:T(1024)S(1)} %copy-done.33, f32[256,1024]{1,0:T(8,128)S(1)} %get-tuple-element.70, f32[1024]{0:T(1024)S(1)} %copy-done.29, f32[1024]{0:T(1024)S(1)} %copy-done.28, f32[256]{0:T(256)S(1)} %add_rsqrt_fusion, ...), kind=kOutput, calls=%fused_computation.5 | convolution fusion | flops 2149842944 | bytes 13658112 | tf_op jit(solution)/shard_map/dot_general | solution.py:22
  111.7 8.8 %convert_reduce_fusion = (f32[4096]{0:T(1024)S(1)}, bf16[256,4096]{1,0:T(8,128)(2,1)S(1)}) fusion(f32[256,4096]{1,0:T(8,128)S(1)} %convolution_add_fusion, bf16[4096,1024]{1,0:T(8,128)(2,1)} %param.26, bf16[1,256,1024]{2,1,0:T(8,128)(2,1)S(1)} %copy-done.26, bf16[256]{0:T(256)(128)(2,1)S(1)} %convert_reduce_fusion.6), kind=kOutput, calls=%fused_computation.13 | convolution fusion | flops 2169761792 | bytes 15221248 | tf_op jit(solution)/shard_map/dot_general | solution.py:26
  120.6 2.7 multiply_reduce_fusion
  123.3 1.5 convert_reduce_fusion.3
  125.0 2.7 fusion.24.dt_ref
  127.8 1.0 copy-done.5
  128.9 1.0 copy-done.7
  129.9 1.0 copy-done.9
  130.9 78.0 %attention_backward.1 = (bf16[1024,256]{1,0:T(8,128)(2,1)S(1)}, bf16[1024,256]{1,0:T(8,128)(2,1)S(1)}, bf16[1024,256]{1,0:T(8,128)(2,1)S(1)}, bf16[3,64,4096]{2,1,0:T(8,128)(2,1)}) custom-call(bf16[1024,256]{1,0:T(8,128)(2,1)S(1)} %fusion.24.dt_ref, bf16[64,4096]{1,0:T(8,128)(2,1)S(1)} %copy-done.5, bf16[64,4096]{1,0:T(8,128)(2,1)S(1)} %copy-done.7, ...), custom_call_target="tpu_custom_call" | custom-call | tf_op jit(solution)/shard_map/attention_backward/pallas_call | solution.py:420
  211.1 2.5 fusion.44
  213.6 1.8 convolution_add_fusion.2
  215.5 2.1 fusion.34
  218.5 1.9 convolution_convert_fusion.2
  220.5 7.1 %convolution_convert_fusion = bf16[1024,4096]{1,0:T(8,128)(2,1)} fusion(bf16[256,4096]{1,0:T(8,128)(2,1)S(1)} %copy-done.21, f32[256,1024]{1,0:T(8,128)} %copy-done.13, f32[1024]{0:T(1024)S(1)} %copy-done.29, f32[1024]{0:T(1024)S(1)} %copy-done.28, f32[256]{0:T(256)S(1)} %add_rsqrt_fusion, f32[256]{0:T(256)S(1)} %broadcast_multiply_fusion.4), kind=kOutput, calls=%fused_computation | convolution fusion | flops 2152988672 | bytes 11544576 | tf_op jit(solution)/shard_map/dot_general | solution.py:26
  227.6 5.5 %convolution_convert_fusion.1 = bf16[4096,1024]{1,0:T(8,128)(2,1)} fusion(bf16[1,256,1024]{2,1,0:T(8,128)(2,1)S(1)} %copy-done.27, bf16[256]{0:T(256)(128)(2,1)S(1)} %convert_reduce_fusion.6, f32[256,4096]{1,0:T(8,128)S(1)} %copy-done.39), kind=kOutput, calls=%fused_computation.1 | convolution fusion | flops 2161377280 | bytes 13107712 | tf_op jit(solution)/shard_map/dot_general | solution.py:26
  233.2 105.5 %halving_sum.1 = (f32[128,1024]{1,0:T(8,128)S(1)}, f32[32,4096]{1,0:T(8,128)S(1)}, f32[32,1024]{1,0:T(8,128)S(1)}) custom-call(bf16[2,4,2,2,128,1024]{5,4,3,2,1,0:T(8,128)(2,1)} %bitcast.110, bf16[2,4,2,2,32,4096]{5,4,3,2,1,0:T(8,128)(2,1)} %bitcast.108, bf16[2,4,2,2,32,1024]{5,4,3,2,1,0:T(8,128)(2,1)S(1)} %bitcast.107), custom_call_target="tpu_custom_call" | custom-call | tf_op jit(solution)/shard_map/halving_sum/pallas_call | solution.py:564
  338.7 1.2 fusion.36
  340.0 5.7 %fusion.26 = bf16[1,256,1024]{2,1,0:T(8,128)(2,1)} fusion(f32[256,1024]{1,0:T(8,128)S(1)} %copy-done.14, bf16[4096,1024]{1,0:T(8,128)(2,1)S(1)} %bitcast.122, f32[1024]{0:T(1024)S(1)} %copy-done.36, f32[256,4096]{1,0:T(8,128)} %copy-done.38), kind=kOutput, calls=%fused_computation.47 | convolution fusion | flops 2157707264 | bytes 14159872 | tf_op jit(solution)/shard_map/dot_general | solution.py:22
  345.7 11.6 %copy.54 = bf16[1024,4096]{1,0:T(8,128)(2,1)} copy(bf16[1024,4096]{0,1:T(8,128)(2,1)} %bitcast.109) | data formatting | bytes 16777216 | tf_op jit(solution)/shard_map/dot_general | solution.py:22
  357.3 6.7 %fusion.45.refs_0_ = f32[32,32,192]{2,1,0:T(8,128)} fusion(bf16[32,32,4096]{2,1,0:T(8,128)(2,1)} %bitcast.111, bf16[192,4096,1]{1,0,2:T(8,128)(2,1)S(1)} %bitcast.123), kind=kOutput, calls=%fused_computation.87 | convolution fusion | flops 1610612736 | bytes 10747904 | tf_op jit(solution)/shard_map/dot_general | solution.py:22
  364.0 28.3 %exchange.1 = (f32[32,32,192]{2,1,0:T(8,128)}, f32[32,8,128]{2,1,0:T(8,128)}) custom-call(f32[32,32,192]{2,1,0:T(8,128)} %fusion.45.refs_0_, f32[32,8,128]{2,1,0:T(8,128)} %bitcast.115), custom_call_target="tpu_custom_call" | custom-call | tf_op jit(solution)/shard_map/exchange/pallas_call | solution.py:630
  394.3 3.8 reshape.159
  398.2 3.5 reduce_sum.190
  401.7 3.8 fusion.41
  406.4 1.1 copy.56
  408.3 1.1 copy.55
  (124 shorter events, 12.6 us)
Async XLA Ops:
  7.2 7.8 %copy-start = (bf16[1024,1024]{1,0:T(8,128)(2,1)S(1)}, bf16[1024,1024]{1,0:T(8,128)(2,1)}, u32[]{:S(2)}) copy-start(bf16[1024,1024]{1,0:T(8,128)(2,1)} %param.23) | copy-start | bytes 6291460
  7.2 7.7 %copy-start.34 = (f32[1024]{0:T(1024)S(1)}, f32[1024]{0:T(1024)}, u32[]{:S(2)}) copy-start(f32[1024]{0:T(1024)} %param.28) | copy-start | bytes 12292
  7.2 338.5 %all-gather.2.cloned.1.call-start = ((), (), s32[]{:S(2)}) async-start(), calls=%async_computation | async-start | bytes 8912896 | tf_op jit(solution)/shard_map/all_gather | solution.py:694
  12.1 5.1 %copy-start.24 = (bf16[256,1024]{1,0:T(8,128)(2,1)S(1)}, bf16[256,1024]{1,0:T(8,128)(2,1)}, u32[]{:S(2)}) copy-start(bf16[256,1024]{1,0:T(8,128)(2,1)} %fusion.28) | copy-start | bytes 1572868
  12.1 5.2 %copy-start.35 = (f32[1024]{0:T(1024)S(1)}, f32[1024]{0:T(1024)}, u32[]{:S(2)}) copy-start(f32[1024]{0:T(1024)} %param.27) | copy-start | bytes 12292
  15.0 89.4 %copy-start.37 = (s32[1,256]{1,0:T(1,128)S(1)}, s32[1,256]{1,0:T(1,128)}, u32[]{:S(2)}) copy-start(s32[1,256]{1,0:T(1,128)} %param.19) | copy-start | bytes 3076
  15.0 89.4 %copy-start.16 = (bf16[1,256,1024]{2,1,0:T(8,128)(2,1)S(1)}, bf16[1,256,1024]{2,1,0:T(8,128)(2,1)}, u32[]{:S(2)}) copy-start(bf16[1,256,1024]{2,1,0:T(8,128)(2,1)} %param.18) | copy-start | bytes 1572868
  15.0 89.4 %copy-start.19 = (bf16[1024,1024]{1,0:T(8,128)(2,1)S(1)}, bf16[1024,1024]{1,0:T(8,128)(2,1)}, u32[]{:S(2)}) copy-start(bf16[1024,1024]{1,0:T(8,128)(2,1)} %param.24) | copy-start | bytes 6291460
  15.0 89.4 %copy-start.30 = (f32[1024]{0:T(1024)S(1)}, f32[1024]{0:T(1024)}, u32[]{:S(2)}) copy-start(f32[1024]{0:T(1024)} %param.29) | copy-start | bytes 12292
  18.3 87.3 %copy-start.28 = (f32[1024]{0:T(1024)S(1)}, f32[1024]{0:T(1024)}, u32[]{:S(2)}) copy-start(f32[1024]{0:T(1024)} %param.34) | copy-start | bytes 12292
  18.3 87.3 %copy-start.29 = (f32[1024]{0:T(1024)S(1)}, f32[1024]{0:T(1024)}, u32[]{:S(2)}) copy-start(f32[1024]{0:T(1024)} %param.35) | copy-start | bytes 12292
  18.3 87.3 %copy-start.33 = (f32[4096]{0:T(1024)S(1)}, f32[4096]{0:T(1024)}, u32[]{:S(2)}) copy-start(f32[4096]{0:T(1024)} %param.30) | copy-start | bytes 49156
  104.3 7.3 %copy-start.2 = (f32[64,4096]{1,0:T(8,128)}, f32[64,4096]{1,0:T(8,128)S(1)}, u32[]{:S(2)}) copy-start(f32[64,4096]{1,0:T(8,128)S(1)} %get-tuple-element.36.o_all) | copy-start | bytes 3145732
  104.3 7.3 %copy-start.4 = (bf16[64,4096]{1,0:T(8,128)(2,1)}, bf16[64,4096]{1,0:T(8,128)(2,1)S(1)}, u32[]{:S(2)}) copy-start(bf16[64,4096]{1,0:T(8,128)(2,1)S(1)} %get-tuple-element.33.q_all) | copy-start | bytes 1572868
  104.4 7.3 %copy-start.6 = (bf16[64,4096]{1,0:T(8,128)(2,1)}, bf16[64,4096]{1,0:T(8,128)(2,1)S(1)}, u32[]{:S(2)}) copy-start(bf16[64,4096]{1,0:T(8,128)(2,1)S(1)} %get-tuple-element.34.k_all) | copy-start | bytes 1572868
  104.4 7.3 %copy-start.8 = (bf16[64,4096]{1,0:T(8,128)(2,1)}, bf16[64,4096]{1,0:T(8,128)(2,1)S(1)}, u32[]{:S(2)}) copy-start(bf16[64,4096]{1,0:T(8,128)(2,1)S(1)} %get-tuple-element.35.v_all) | copy-start | bytes 1572868
  105.3 18.0 %copy-start.13 = (f32[256,1024]{1,0:T(8,128)}, f32[256,1024]{1,0:T(8,128)S(1)}, u32[]{:S(2)}) copy-start(f32[256,1024]{1,0:T(8,128)S(1)} %get-tuple-element.70) | copy-start | bytes 3145732
  105.6 6.1 %copy-start.26 = (bf16[1,256,1024]{2,1,0:T(8,128)(2,1)S(1)}, bf16[1,256,1024]{2,1,0:T(8,128)(2,1)}, u32[]{:S(2)}) copy-start(bf16[1,256,1024]{2,1,0:T(8,128)(2,1)} %param.20) | copy-start | bytes 1572868
  105.6 15.0 %slice-start = ((s8[8388608]{0:T(1024)(128)(4,1)}), s8[4194304]{0:T(1024)(128)(4,1)S(1)}, s32[]{:S(2)}) async-start(s8[8388608]{0:T(1024)(128)(4,1)} %bitcast.119), calls=%async_computation.1 | async-start | bytes 8388608
  111.7 8.8 %copy-start.38 = (f32[256,4096]{1,0:T(8,128)}, f32[256,4096]{1,0:T(8,128)S(1)}, u32[]{:S(2)}) copy-start(f32[256,4096]{1,0:T(8,128)S(1)} %convolution_add_fusion) | copy-start | bytes 12582916
  111.7 8.8 %slice-start.1 = ((s8[8388608]{0:T(1024)(128)(4,1)}), s8[4194304]{0:T(1024)(128)(4,1)S(1)}, s32[]{:S(2)}) async-start(s8[8388608]{0:T(1024)(128)(4,1)} %bitcast.119), calls=%async_computation.2 | async-start | bytes 8388608
  220.5 7.1 %copy-start.27 = (bf16[1,256,1024]{2,1,0:T(8,128)(2,1)S(1)}, bf16[1,256,1024]{2,1,0:T(8,128)(2,1)}, u32[]{:S(2)}) copy-start(bf16[1,256,1024]{2,1,0:T(8,128)(2,1)} %param.20) | copy-start | bytes 1572868
  220.5 7.1 %copy-start.39 = (f32[256,4096]{1,0:T(8,128)S(1)}, f32[256,4096]{1,0:T(8,128)}, u32[]{:S(2)}) copy-start(f32[256,4096]{1,0:T(8,128)} %copy-done.38) | copy-start | bytes 12582916
  220.5 119.4 %slice-start.2 = ((s8[8388608]{0:T(1024)(128)(4,1)}), s8[4194304]{0:T(1024)(128)(4,1)S(1)}, s32[]{:S(2)}) async-start(s8[8388608]{0:T(1024)(128)(4,1)} %bitcast.121), calls=%async_computation.3 | async-start | bytes 8388608
  227.6 112.3 %slice-start.3 = ((s8[8388608]{0:T(1024)(128)(4,1)}), s8[4194304]{0:T(1024)(128)(4,1)S(1)}, s32[]{:S(2)}) async-start(s8[8388608]{0:T(1024)(128)(4,1)} %bitcast.121), calls=%async_computation.4 | async-start | bytes 8388608
  233.1 105.6 %copy-start.15 = (f32[256,1024]{1,0:T(8,128)S(1)}, f32[256,1024]{1,0:T(8,128)}, u32[]{:S(2)}) copy-start(f32[256,1024]{1,0:T(8,128)} %get-tuple-element.56) | copy-start | bytes 3145732
  233.1 105.6 %copy-start.18 = (bf16[1,256,1024]{2,1,0:T(8,128)(2,1)S(1)}, bf16[1,256,1024]{2,1,0:T(8,128)(2,1)}, u32[]{:S(2)}) copy-start(bf16[1,256,1024]{2,1,0:T(8,128)(2,1)} %param.18) | copy-start | bytes 1572868
  233.1 105.6 %copy-start.25 = (f32[256,1024]{1,0:T(8,128)S(1)}, f32[256,1024]{1,0:T(8,128)}, u32[]{:S(2)}) copy-start(f32[256,1024]{1,0:T(8,128)} %get-tuple-element.72) | copy-start | bytes 3145732
  233.1 106.8 %copy-start.14 = (f32[256,1024]{1,0:T(8,128)S(1)}, f32[256,1024]{1,0:T(8,128)}, u32[]{:S(2)}) copy-start(f32[256,1024]{1,0:T(8,128)} %copy-done.13) | copy-start | bytes 3145732
  233.1 106.8 %copy-start.36 = (f32[1024]{0:T(1024)S(1)}, f32[1024]{0:T(1024)}, u32[]{:S(2)}) copy-start(f32[1024]{0:T(1024)} %param.31) | copy-start | bytes 12292
  345.7 11.6 %copy-start.32 = (bf16[3,64,4096]{2,1,0:T(8,128)(2,1)S(1)}, bf16[3,64,4096]{2,1,0:T(8,128)(2,1)}, u32[]{:S(2)}) copy-start(bf16[3,64,4096]{2,1,0:T(8,128)(2,1)} %get-tuple-element.41) | copy-start | bytes 4718596
  394.3 18.1 %copy-start.1 = (bf16[1024,1024]{1,0:T(8,128)(2,1)S(1)}, bf16[1024,1024]{1,0:T(8,128)(2,1)}, u32[]{:S(2)}) copy-start(bf16[1024,1024]{1,0:T(8,128)(2,1)} %param.23) | copy-start | bytes 6291460
  (13 other events, 33.9 us)
Sparse Core Ops, SparseCore 0:
  12.2 111.3 all-gather.1

commit v2 on v1

--- a/solution.py
+++ b/solution.py
@@ -241,6 +241,139 @@
     )(q_t, k_t, v_t)
 
 
+CHUNKS = 9
+TICKS = CHUNKS + 4
+
+
+def halving_plan(sources, own, got0, got1a, got1b, got2, got3, got4, total, sems):
+    load_sem, send_sem, recv_sem = sems
+    me = lax.axis_index("seq")
+    x = lax.axis_index("scene")
+    core = lax.rem(me, 2)
+    y = lax.rem(me // 2, 2)
+    z0 = lax.rem(me // 4, 2)
+    z1 = me // 8
+    at_core = (x, me + 1 - 2 * core)
+    at_x = (1 - x, me)
+    at_y = (x, me + 2 - 4 * y)
+    at_z0 = (x, me + 4 - 8 * z0)
+    at_z1 = (x, me + 8 - 16 * z1)
+    top, low = slice(0, 16), slice(16, 32)
+
+    def copy_of(slot, c):
+        src, dst, device = (
+            lambda: (got0.at[c], got0.at[c], at_core),
+            lambda: (own.at[c, 1 - x, :, :, top, :], got1a.at[c], at_x),
+            lambda: (own.at[c, :, :, 1 - y, low, :], got1b.at[c], at_y),
+            lambda: (got1a.at[c, :, 1 - y], got2.at[c, :, top, :], at_y),
+            lambda: (got1b.at[c, 1 - x], got2.at[c, :, low, :], at_x),
+            lambda: (got2.at[c, 1 - z0], got3.at[c, 0], at_z0),
+            lambda: (got2.at[c, 3 - z0], got3.at[c, 1], at_z0),
+            lambda: (got3.at[c, 1 - z1], got4.at[c], at_z1),
+        )[slot]()
+        return remote(src, dst, send_sem.at[c, slot], recv_sem.at[c, slot], device)
+
+    def first_copies(c):
+        ref, rows, columns = sources[c]
+        load = pltpu.make_async_copy(
+            ref.at[:, :, :, core, rows, columns], own.at[c], load_sem.at[c]
+        )
+        over = remote(
+            ref.at[:, :, :, 1 - core, rows, columns],
+            got0.at[c],
+            send_sem.at[c, 0],
+            recv_sem.at[c, 0],
+            at_core,
+        )
+        return load, over
+
+    def begin():
+        for c in range(CHUNKS):
+            for copy in first_copies(c):
+                copy.start()
+
+    def stage1(c):
+        pltpu.make_async_copy(own.at[c], own.at[c], load_sem.at[c]).wait()
+        copy_of(0, c).wait_recv()
+        own[c] = own[c] + got0[c]
+        copy_of(1, c).start()
+        copy_of(2, c).start()
+
+    def stage2(c):
+        copy_of(1, c).wait_recv()
+        got1a[c] = own[c, x, :, :, top, :] + got1a[c]
+        copy_of(3, c).start()
+        copy_of(2, c).wait_recv()
+        got1b[c] = own[c, :, :, y, low, :] + got1b[c]
+        copy_of(4, c).start()
+
+    def stage3(c):
+        copy_of(3, c).wait_recv()
+        got2[c, :, top, :] = got1a[c, :, y] + got2[c, :, top, :]
+        copy_of(4, c).wait_recv()
+        got2[c, :, low, :] = got1b[c, x] + got2[c, :, low, :]
+        copy_of(5, c).start()
+        copy_of(6, c).start()
+
+    def stage4(c):
+        copy_of(5, c).wait_recv()
+        copy_of(6, c).wait_recv()
+        got3[c, 0] = got2[c, z0] + got3[c, 0]
+        got3[c, 1] = got2[c, 2 + z0] + got3[c, 1]
+        copy_of(7, c).start()
+
+    def stage5(c):
+        copy_of(7, c).wait_recv()
+        total[c] = got3[c, z1].astype(f32) + got4[c].astype(f32)
+
+    stages = (stage1, stage2, stage3, stage4, stage5)
+
+    def tick(when):
+        for depth in reversed(range(len(stages))):
+            c = when - depth
+
+            @pl.when((c >= 0) & (c < CHUNKS))
+            def _(stage=stages[depth], c=c):
+                stage(c)
+
+    def finish(sinks):
+        for c, (ref, rows, columns) in enumerate(sinks):
+            pltpu.make_async_copy(total.at[c], ref.at[rows, columns], load_sem.at[c]).start()
+        for c in range(CHUNKS):
+            for slot in range(8):
+                copy_of(slot, c).wait_send()
+        for c, (ref, rows, columns) in enumerate(sinks):
+            pltpu.make_async_copy(total.at[c], ref.at[rows, columns], load_sem.at[c]).wait()
+
+    return [at_core, at_x, at_y, at_z0, at_z1], begin, tick, finish
+
+
+def halving_pieces(down, up, out):
+    every = slice(None)
+    return (
+        [(down, slice(32 * i, 32 * i + 32), every) for i in range(4)]
+        + [(up, every, slice(1024 * i, 1024 * i + 1024)) for i in range(4)]
+        + [(out, every, every)]
+    )
+
+
+def halving_scratch():
+    dma = pltpu.SemaphoreType.DMA
+    return [
+        pltpu.VMEM((CHUNKS, 2, 4, 2, 32, 1024), bf16),
+        pltpu.VMEM((CHUNKS, 2, 4, 2, 32, 1024), bf16),
+        pltpu.VMEM((CHUNKS, 4, 2, 16, 1024), bf16),
+        pltpu.VMEM((CHUNKS, 2, 4, 16, 1024), bf16),
+        pltpu.VMEM((CHUNKS, 4, 32, 1024), bf16),
+        pltpu.VMEM((CHUNKS, 2, 32, 1024), bf16),
+        pltpu.VMEM((CHUNKS, 32, 1024), bf16),
+        pltpu.VMEM((CHUNKS, 32, 1024), f32),
+        dma((CHUNKS,)),
+        dma((CHUNKS, 8)),
+        dma((CHUNKS, 8)),
+    ]
+
+
 def backward_kernel(
     n,
     tok,
@@ -250,10 +383,16 @@
     v_all,
     o_all,
     lse_all,
+    down_ref,
+    up_ref,
+    out_ref,
     dq_ref,
     dk_ref,
     dv_ref,
     heads_ref,
+    down_sum,
+    up_sum,
+    out_sum,
     d_all,
     q_nat,
     k_nat,
@@ -272,6 +411,7 @@
     q_recv,
     q_local,
     save_sem,
+    *halving,
 ):
     me = lax.axis_index("seq")
     scene = lax.axis_index("scene")
@@ -279,7 +419,10 @@
     chips = n // 2
     length = n * tok
     wide = 2 * tok
-    greet([(scene, lax.rem(me + j, n)) for j in range(1, n)])
+    partners, begin, tick, finish = halving_plan(
+        halving_pieces(down_ref, up_ref, out_ref), *halving[:8], halving[8:]
+    )
+    greet([(scene, lax.rem(me + j, n)) for j in range(1, n)] + [partners[1]])
 
     def rows(head):
         return pl.ds(pl.multiple_of(head * HEAD_DIM, HEAD_DIM), HEAD_DIM)
@@ -302,6 +445,7 @@
         copies[-1].start()
     local = pltpu.make_async_copy(dt_ref.at[rows(me), :], d_all.at[:, lanes(me)], in_local)
     local.start()
+    begin()
     q_nat[...] = q_all[...].T
     k_nat[...] = k_all[...].T
     v_nat[...] = v_all[...].T
@@ -374,6 +518,7 @@
         low[1, :, span] = dk.astype(bf16).T
         low[2, :, span] = dv.astype(bf16).T
 
+    tick(0)
     keys(0, False)
     mine[1].start()
     mine[2].start()
@@ -386,15 +531,24 @@
             kv_copy(a, step, 1).start()
 
     def step_body(step, carry):
+        tick(step)
         keys(step, False)
         send_kv(step)
         return carry
 
     lax.fori_loop(1, chips - 1, step_body, 0)
+    tick(chips - 1)
     keys(chips - 1, True)
     send_kv(chips - 1)
     save = pltpu.make_async_copy(low, heads_ref, save_sem)
     save.start()
+
+    def tick_body(when, carry):
+        tick(when)
+        return carry
+
+    lax.fori_loop(chips, TICKS, tick_body, 0)
+    finish(halving_pieces(down_sum, up_sum, out_sum))
     for copy in copies:
         copy.wait_send()
     for copy in mine:
@@ -409,7 +563,8 @@
     save.wait()
 
 
-def attention_backward(n, d_t, q_all, k_all, v_all, o_all, lse_all):
+def attention_backward(n, d_t, q_all, k_all, v_all, o_all, lse_all, *weights):
+    shards = 32
     tok = d_t.shape[1]
     length = n * tok
     chips = n // 2
@@ -419,9 +574,10 @@
     part = jax.ShapeDtypeStruct(d_t.shape, bf16)
     return pl.pallas_call(
         functools.partial(backward_kernel, n, tok),
-        out_shape=(part, part, part, jax.ShapeDtypeStruct((3, HEAD_DIM, length), bf16)),
-        in_specs=[any_spec] + [vmem] * 5,
-        out_specs=[any_spec] * 4,
+        out_shape=(part, part, part, jax.ShapeDtypeStruct((3, HEAD_DIM, length), bf16))
+        + tuple(jax.ShapeDtypeStruct((w.shape[0] // shards, w.shape[1]), f32) for w in weights),
+        in_specs=[any_spec] + [vmem] * 5 + [any_spec] * 3,
+        out_specs=[any_spec] * 7,
         scratch_shapes=[
             pltpu.VMEM((HEAD_DIM, length), bf16),
             pltpu.VMEM((length, HEAD_DIM), bf16),
@@ -441,150 +597,21 @@
             dma((chips, 2)),
             dma,
             dma,
-        ],
+        ]
+        + halving_scratch(),
         compiler_params=pltpu.CompilerParams(
-            collective_id=1, has_side_effects=True, vmem_limit_bytes=48 << 20
+            collective_id=1, has_side_effects=True, vmem_limit_bytes=60 << 20
         ),
         name="attention_backward",
-    )(d_t, q_all, k_all, v_all, o_all, lse_all)
-
-
-def halving_kernel(
-    down_ref,
-    up_ref,
-    out_ref,
-    down_sum,
-    up_sum,
-    out_sum,
-    own,
-    got0,
-    got1a,
-    got1b,
-    got2,
-    got3,
-    got4,
-    load_sem,
-    send_sem,
-    recv_sem,
-):
-    me = lax.axis_index("seq")
-    x = lax.axis_index("scene")
-    core = lax.rem(me, 2)
-    y = lax.rem(me // 2, 2)
-    z0 = lax.rem(me // 4, 2)
-    z1 = me // 8
-    at_core = (x, me + 1 - 2 * core)
-    at_x = (1 - x, me)
-    at_y = (x, me + 2 - 4 * y)
-    at_z0 = (x, me + 4 - 8 * z0)
-    at_z1 = (x, me + 8 - 16 * z1)
-    greet([at_core, at_x, at_y, at_z0, at_z1])
-
-    every = slice(None)
-    pieces = (
-        [(down_ref, down_sum, slice(32 * i, 32 * i + 32), every) for i in range(4)]
-        + [(up_ref, up_sum, every, slice(1024 * i, 1024 * i + 1024)) for i in range(4)]
-        + [(out_ref, out_sum, every, every)]
-    )
-    top, low = slice(0, 16), slice(16, 32)
-    started = []
-    flight = {}
-
-    def send(src, dst, chunk, slot, device):
-        copy = remote(src, dst, send_sem.at[chunk, slot], recv_sem.at[chunk, slot], device)
-        copy.start()
-        started.append(copy)
-        return copy
-
-    for c, (ref, _, rows, columns) in enumerate(pieces):
-        load = pltpu.make_async_copy(
-            ref.at[:, :, :, core, rows, columns], own.at[c], load_sem.at[c]
-        )
-        load.start()
-        flight[c, 0] = (
-            load,
-            send(ref.at[:, :, :, 1 - core, rows, columns], got0.at[c], c, 0, at_core),
-        )
-
-    def stage1(c):
-        flight[c, 0][0].wait()
-        flight[c, 0][1].wait_recv()
-        own[c] = own[c] + got0[c]
-        flight[c, 1] = (
-            send(own.at[c, 1 - x, :, :, top, :], got1a.at[c], c, 1, at_x),
-            send(own.at[c, :, :, 1 - y, low, :], got1b.at[c], c, 2, at_y),
-        )
-
-    def stage2(c):
-        flight[c, 1][0].wait_recv()
-        got1a[c] = own[c, x, :, :, top, :] + got1a[c]
-        first = send(got1a.at[c, :, 1 - y], got2.at[c, :, top, :], c, 3, at_y)
-        flight[c, 1][1].wait_recv()
-        got1b[c] = own[c, :, :, y, low, :] + got1b[c]
-        flight[c, 2] = (first, send(got1b.at[c, 1 - x], got2.at[c, :, low, :], c, 4, at_x))
-
-    def stage3(c):
-        flight[c, 2][0].wait_recv()
-        got2[c, :, top, :] = got1a[c, :, y] + got2[c, :, top, :]
-        flight[c, 2][1].wait_recv()
-        got2[c, :, low, :] = got1b[c, x] + got2[c, :, low, :]
-        flight[c, 3] = (
-            send(got2.at[c, 1 - z0], got3.at[c, 0], c, 5, at_z0),
-            send(got2.at[c, 3 - z0], got3.at[c, 1], c, 6, at_z0),
-        )
-
-    def stage4(c):
-        flight[c, 3][0].wait_recv()
-        flight[c, 3][1].wait_recv()
-        got3[c, 0] = got2[c, z0] + got3[c, 0]
-        got3[c, 1] = got2[c, 2 + z0] + got3[c, 1]
-        flight[c, 4] = (send(got3.at[c, 1 - z1], got4.at[c], c, 7, at_z1),)
-
-    def stage5(c):
-        flight[c, 4][0].wait_recv()
-        _, ref, rows, columns = pieces[c]
-        ref[rows, columns] = got3[c, z1].astype(f32) + got4[c].astype(f32)
-
-    stages = (stage1, stage2, stage3, stage4, stage5)
-    for tick in range(len(pieces) + len(stages) - 1):
-        for depth in reversed(range(len(stages))):
-            if 0 <= tick - depth < len(pieces):
-                stages[depth](tick - depth)
-    for copy in started:
-        copy.wait_send()
-
-
-def halving_sum(down, up, out):
-    shards = 32
-    any_spec = pl.BlockSpec(memory_space=pl.ANY)
-    vmem = pl.BlockSpec(memory_space=pltpu.VMEM)
-    dma = pltpu.SemaphoreType.DMA
-    arrays = [down, up, out]
-    chunks = 9
-    return pl.pallas_call(
-        halving_kernel,
-        out_shape=tuple(
-            jax.ShapeDtypeStruct((a.shape[0] // shards, a.shape[1]), f32) for a in arrays
-        ),
-        in_specs=[any_spec] * 3,
-        out_specs=[vmem] * 3,
-        scratch_shapes=[
-            pltpu.VMEM((chunks, 2, 4, 2, 32, 1024), bf16),
-            pltpu.VMEM((chunks, 2, 4, 2, 32, 1024), bf16),
-            pltpu.VMEM((chunks, 4, 2, 16, 1024), bf16),
-            pltpu.VMEM((chunks, 2, 4, 16, 1024), bf16),
-            pltpu.VMEM((chunks, 4, 32, 1024), bf16),
-            pltpu.VMEM((chunks, 2, 32, 1024), bf16),
-            pltpu.VMEM((chunks, 32, 1024), bf16),
-            dma((chunks,)),
-            dma((chunks, 8)),
-            dma((chunks, 8)),
-        ],
-        compiler_params=pltpu.CompilerParams(
-            collective_id=2, has_side_effects=True, vmem_limit_bytes=48 << 20
-        ),
-        name="halving_sum",
-    )(*(a.reshape(2, 4, 2, 2, a.shape[0] // shards, a.shape[1]) for a in arrays))
+    )(
+        d_t,
+        q_all,
+        k_all,
+        v_all,
+        o_all,
+        lse_all,
+        *(w.reshape(2, 4, 2, 2, w.shape[0] // shards, w.shape[1]) for w in weights),
+    )
 
 
 def exchange_kernel(scenes, n, count, *refs):
@@ -721,9 +748,8 @@
     grad_bout = jnp.sum(resid_low.astype(f32), axis=0)
     att_grad_t = matmul_nt(w_out, resid_low).astype(bf16)
 
-    sum_down, sum_up, sum_out = halving_sum(grad_down, grad_up, grad_out)
-    dq_t, dk_t, dv_t, heads_t = attention_backward(
-        n, att_grad_t, q_all, k_all, v_all, o_all, lse_all
+    dq_t, dk_t, dv_t, heads_t, sum_down, sum_up, sum_out = attention_backward(
+        n, att_grad_t, q_all, k_all, v_all, o_all, lse_all, grad_down, grad_up, grad_out
     )
 
     head_grads = matmul(heads_t.reshape(3 * HEAD_DIM, n * tok), normed_all)

time: 425 us -> 385 us (0.906)
  Pallas kernels: 298 us -> 258 us
  local copies, waits for them, and re-layouts: 33.5 us -> 26.2 us
  matrix products: 60.5 us -> 65.4 us
    pallas_call x1 -> x0, Pallas kernels: 106 us -> none  [halving_sum(): pl.pallas_call(halving_kernel, out_shape=tuple((jax.ShapeDtypeStruct((a.s...]
    pallas_call x1, Pallas kernels: 78 us -> 140 us  [attention_backward(): pl.pallas_call(functools.partial(backward_kernel, n, tok), out_shape=(par...]
    pallas_call x1, Pallas kernels: 86 us -> 90.5 us  [attention_forward(): pl.pallas_call(functools.partial(forward_kernel, n, tok), out_shape=(jax....]
  transfers between devices with their start and end apart: 1 -> 1, of which waited for: 0 -> 0; matrix products, arithmetic and copies ran while one was open for 14% -> 17% of each run, Pallas kernels for 64% -> 61%
where the time goes in v2:
time: 385 us; the launch traced here: 379 us
  Pallas kernels  258 us (67%)
  matrix products  65.4 us (17%)
  local copies, waits for them, and re-layouts  26.2 us (7%)
  between operations  14.8 us (4%)
  other arithmetic  14.5 us (4%)
    pallas_call x1, Pallas kernels, attention_backward(): pl.pallas_call(functools.partial(backward_kernel, n, tok), out_shape=(par...  140 us
    pallas_call x1, Pallas kernels, attention_forward(): pl.pallas_call(functools.partial(forward_kernel, n, tok), out_shape=(jax....  90.5 us
    dot_general x12, matrix products, contract(): lax.dot_general(left, right, (((left_dim,), (right_dim,)), ((), ())), pre...  42.1 us
    pallas_call x1, Pallas kernels, exchange(): pl.pallas_call(functools.partial(exchange_kernel, scenes, n, count), out_...  28 us
    dot_general x4, matrix products, matmul(): return jnp.dot(left, right, preferred_element_type=jnp.float32)  23.3 us
    dot_general x1, local copies, waits for them, and re-layouts, matmul(): return jnp.dot(left, right, preferred_element_type=jnp.float32)  11.7 us
  transfers between devices with their start and end apart: 1, of which 0 were waited for; matrix products, arithmetic and copies ran while one was open for 17% of the time, Pallas kernels for 61%

profile of v2, /device:TPU:0, one launch (start us, length us, event | category | flops | bytes accessed | tf_op | source)
XLA Modules:
  0.0 379.0 jit_solution(18401467687271392704)
XLA Ops:
  7.3 1.3 convert_reduce_fusion.2
  8.6 1.3 fusion.35
  9.9 2.1 fusion.28
  12.1 2.7 fusion.23.kt_ref
  14.9 2.9 fusion.25.qt_ref
  17.8 1.0 fusion.22.vt_ref
  18.9 90.5 %attention_forward.1 = (bf16[1024,256]{1,0:T(8,128)(2,1)S(1)}, bf16[64,4096]{1,0:T(8,128)(2,1)S(1)}, bf16[64,4096]{1,0:T(8,128)(2,1)S(1)}, bf16[64,4096]{1,0:T(8...) custom-call(bf16[1024,256]{1,0:T(8,128)(2,1)S(1)} %fusion.25.qt_ref, bf16[1024,256]{1,0:T(8,128)(2,1)S(1)} %fusion.23.kt_ref, ...), custom_call_target="tpu_custom_call" | custom-call | tf_op jit(solution)/shard_map/attention_forward/pallas_call | solution.py:209
  109.5 0.8 fusion.43
  110.7 5.9 %convolution_add_fusion = f32[256,4096]{1,0:T(8,128)S(1)} fusion(bf16[1024,4096]{1,0:T(8,128)(2,1)} %param.25, f32[4096]{0:T(1024)S(1)} %copy-done.20, f32[256,1024]{1,0:T(8,128)S(1)} %get-tuple-element.70, f32[1024]{0:T(1024)S(1)} %copy-done.17, f32[1024]{0:T(1024)S(1)} %copy-done.16, f32[256]{0:T(256)S(1)} %add_rsqrt_fusion, ...), kind=kOutput, calls=%fused_computation.5 | convolution fusion | flops 2149842944 | bytes 13658112 | tf_op jit(solution)/shard_map/dot_general | solution.py:22
  116.6 8.9 %convert_reduce_fusion = (f32[4096]{0:T(1024)S(1)}, bf16[256,4096]{1,0:T(8,128)(2,1)S(1)}) fusion(f32[256,4096]{1,0:T(8,128)S(1)} %convolution_add_fusion, bf16[4096,1024]{1,0:T(8,128)(2,1)} %param.26, bf16[1,256,1024]{2,1,0:T(8,128)(2,1)S(1)} %copy-done.14, bf16[256]{0:T(256)(128)(2,1)S(1)} %convert_reduce_fusion.6), kind=kOutput, calls=%fused_computation.13 | convolution fusion | flops 2169761792 | bytes 15221248 | tf_op jit(solution)/shard_map/dot_general | solution.py:26
  125.6 6.3 %multiply_reduce_fusion = (f32[1024]{0:T(1024)S(1)}, f32[256]{0:T(256)S(1)}, f32[256]{0:T(256)S(1)}, f32[1024]{0:T(1024)S(1)}, f32[256,1024]{1,0:T(8,128)S(1)}) fusion(f32[256,1024]{1,0:T(8,128)S(1)} %get-tuple-element.70, f32[256]{0:T(256)S(1)} %add_rsqrt_fusion, f32[256]{0:T(256)S(1)} %broadcast_multiply_fusion.4, f32[1024]{0:T(1024)S(1)} %copy-done.16, ...), kind=kOutput, calls=%fused_computation.57 | convolution fusion | flops 2149840384 | bytes 12599296 | tf_op jit(solution)/shard_map/dot_general | solution.py:26
  132.4 1.5 fusion.24.dt_ref
  134.0 2.1 convolution_convert_fusion.2
  136.1 5.7 %convolution_convert_fusion = bf16[1024,4096]{1,0:T(8,128)(2,1)} fusion(bf16[256,4096]{1,0:T(8,128)(2,1)S(1)} %get-tuple-element.74, f32[256,1024]{1,0:T(8,128)S(1)} %get-tuple-element.70, f32[1024]{0:T(1024)S(1)} %copy-done.17, f32[1024]{0:T(1024)S(1)} %copy-done.16, f32[256]{0:T(256)S(1)} %add_rsqrt_fusion, f32[256]{0:T(256)S(1)} %broadcast_multiply_fusion.4), kind=kOutput, calls=%fused_computation | convolution fusion | flops 2152988672 | bytes 11544576 | tf_op jit(solution)/shard_map/dot_general | solution.py:26
  141.8 5.4 %convolution_convert_fusion.1 = bf16[4096,1024]{1,0:T(8,128)(2,1)} fusion(bf16[1,256,1024]{2,1,0:T(8,128)(2,1)S(1)} %copy-done.14, bf16[256]{0:T(256)(128)(2,1)S(1)} %convert_reduce_fusion.6, f32[256,4096]{1,0:T(8,128)S(1)} %convolution_add_fusion), kind=kOutput, calls=%fused_computation.1 | convolution fusion | flops 2161377280 | bytes 13107712 | tf_op jit(solution)/shard_map/dot_general | solution.py:26
  147.3 139.5 %attention_backward.1 = (bf16[1024,256]{1,0:T(8,128)(2,1)}, bf16[1024,256]{1,0:T(8,128)(2,1)}, bf16[1024,256]{1,0:T(8,128)(2,1)}, bf16[3,64,4096]{2,1,0:T(8,128)...) custom-call(bf16[1024,256]{1,0:T(8,128)(2,1)} %fusion.24.dt_ref, bf16[64,4096]{1,0:T(8,128)(2,1)} %copy-done.2, ...), custom_call_target="tpu_custom_call" | custom-call | tf_op jit(solution)/shard_map/attention_backward/pallas_call | solution.py:575
  286.8 1.3 convert_reduce_fusion.5
  288.1 1.3 convert_reduce_fusion.4
  289.6 2.6 fusion.44
  292.3 1.8 convolution_add_fusion.2
  294.2 2.1 fusion.34
  297.4 2.9 fusion.36
  300.3 8.2 %fusion.26 = bf16[1,256,1024]{2,1,0:T(8,128)(2,1)} fusion(f32[256,1024]{1,0:T(8,128)S(1)} %get-tuple-element.70, bf16[4096,1024]{1,0:T(8,128)(2,1)} %param.26, f32[1024]{0:T(1024)S(1)} %copy-done.23, f32[256,4096]{1,0:T(8,128)} %copy-done.25), kind=kOutput, calls=%fused_computation.47 | convolution fusion | flops 2157707264 | bytes 14159872 | tf_op jit(solution)/shard_map/dot_general | solution.py:22
  308.5 11.7 %copy.54 = bf16[1024,4096]{1,0:T(8,128)(2,1)} copy(bf16[1024,4096]{0,1:T(8,128)(2,1)} %bitcast.108) | data formatting | bytes 16777216 | tf_op jit(solution)/shard_map/dot_general | solution.py:22
  320.2 7.1 %fusion.45.refs_0_ = f32[32,32,192]{2,1,0:T(8,128)} fusion(bf16[32,32,4096]{2,1,0:T(8,128)(2,1)} %bitcast.110, bf16[192,4096,1]{1,0,2:T(8,128)(2,1)} %bitcast.119), kind=kOutput, calls=%fused_computation.87 | convolution fusion | flops 1610612736 | bytes 10747904 | tf_op jit(solution)/shard_map/dot_general | solution.py:22
  327.4 28.0 %exchange.1 = (f32[32,32,192]{2,1,0:T(8,128)}, f32[32,8,128]{2,1,0:T(8,128)}) custom-call(f32[32,32,192]{2,1,0:T(8,128)} %fusion.45.refs_0_, f32[32,8,128]{2,1,0:T(8,128)} %bitcast.115), custom_call_target="tpu_custom_call" | custom-call | tf_op jit(solution)/shard_map/exchange/pallas_call | solution.py:657
  355.4 0.9 reduce_sum.191
  357.5 3.5 reshape.162
  361.0 2.5 reduce_sum.190
  363.5 1.2 fusion.41
  365.7 1.1 copy.56
  369.2 1.9 copy.67
  (85 shorter events, 7.7 us)
Async XLA Ops:
  7.2 10.6 %copy-start = (bf16[1024,1024]{1,0:T(8,128)(2,1)S(1)}, bf16[1024,1024]{1,0:T(8,128)(2,1)}, u32[]{:S(2)}) copy-start(bf16[1024,1024]{1,0:T(8,128)(2,1)} %param.23) | copy-start | bytes 6291460
  7.2 7.6 %copy-start.21 = (f32[1024]{0:T(1024)S(1)}, f32[1024]{0:T(1024)}, u32[]{:S(2)}) copy-start(f32[1024]{0:T(1024)} %param.27) | copy-start | bytes 12292
  7.2 301.3 %all-gather.2.cloned.1.call-start = ((), (), s32[]{:S(2)}) async-start(), calls=%async_computation | async-start | bytes 8912896 | tf_op jit(solution)/shard_map/all_gather | solution.py:721
  12.1 5.7 %copy-start.11 = (bf16[256,1024]{1,0:T(8,128)(2,1)S(1)}, bf16[256,1024]{1,0:T(8,128)(2,1)}, u32[]{:S(2)}) copy-start(bf16[256,1024]{1,0:T(8,128)(2,1)} %fusion.28) | copy-start | bytes 1572868
  12.1 5.8 %copy-start.22 = (f32[1024]{0:T(1024)S(1)}, f32[1024]{0:T(1024)}, u32[]{:S(2)}) copy-start(f32[1024]{0:T(1024)} %param.28) | copy-start | bytes 12292
  14.8 94.6 %copy-start.24 = (s32[1,256]{1,0:T(1,128)S(1)}, s32[1,256]{1,0:T(1,128)}, u32[]{:S(2)}) copy-start(s32[1,256]{1,0:T(1,128)} %param.19) | copy-start | bytes 3076
  14.9 94.6 %copy-start.7 = (bf16[1,256,1024]{2,1,0:T(8,128)(2,1)S(1)}, bf16[1,256,1024]{2,1,0:T(8,128)(2,1)}, u32[]{:S(2)}) copy-start(bf16[1,256,1024]{2,1,0:T(8,128)(2,1)} %param.18) | copy-start | bytes 1572868
  14.9 94.6 %copy-start.9 = (bf16[1024,1024]{1,0:T(8,128)(2,1)S(1)}, bf16[1024,1024]{1,0:T(8,128)(2,1)}, u32[]{:S(2)}) copy-start(bf16[1024,1024]{1,0:T(8,128)(2,1)} %param.24) | copy-start | bytes 6291460
  14.9 94.6 %copy-start.18 = (f32[1024]{0:T(1024)S(1)}, f32[1024]{0:T(1024)}, u32[]{:S(2)}) copy-start(f32[1024]{0:T(1024)} %param.29) | copy-start | bytes 12292
  18.8 91.8 %copy-start.16 = (f32[1024]{0:T(1024)S(1)}, f32[1024]{0:T(1024)}, u32[]{:S(2)}) copy-start(f32[1024]{0:T(1024)} %param.34) | copy-start | bytes 12292
  18.8 91.8 %copy-start.17 = (f32[1024]{0:T(1024)S(1)}, f32[1024]{0:T(1024)}, u32[]{:S(2)}) copy-start(f32[1024]{0:T(1024)} %param.35) | copy-start | bytes 12292
  18.9 91.8 %copy-start.20 = (f32[4096]{0:T(1024)S(1)}, f32[4096]{0:T(1024)}, u32[]{:S(2)}) copy-start(f32[4096]{0:T(1024)} %param.30) | copy-start | bytes 49156
  109.4 7.1 %copy-start.1 = (f32[64,4096]{1,0:T(8,128)}, f32[64,4096]{1,0:T(8,128)S(1)}, u32[]{:S(2)}) copy-start(f32[64,4096]{1,0:T(8,128)S(1)} %get-tuple-element.36.o_all) | copy-start | bytes 3145732
  109.4 7.1 %copy-start.2 = (bf16[64,4096]{1,0:T(8,128)(2,1)}, bf16[64,4096]{1,0:T(8,128)(2,1)S(1)}, u32[]{:S(2)}) copy-start(bf16[64,4096]{1,0:T(8,128)(2,1)S(1)} %get-tuple-element.33.q_all) | copy-start | bytes 1572868
  109.4 7.1 %copy-start.3 = (bf16[64,4096]{1,0:T(8,128)(2,1)}, bf16[64,4096]{1,0:T(8,128)(2,1)S(1)}, u32[]{:S(2)}) copy-start(bf16[64,4096]{1,0:T(8,128)(2,1)S(1)} %get-tuple-element.34.k_all) | copy-start | bytes 1572868
  109.5 7.1 %copy-start.4 = (bf16[64,4096]{1,0:T(8,128)(2,1)}, bf16[64,4096]{1,0:T(8,128)(2,1)S(1)}, u32[]{:S(2)}) copy-start(bf16[64,4096]{1,0:T(8,128)(2,1)S(1)} %get-tuple-element.35.v_all) | copy-start | bytes 1572868
  109.5 7.1 %copy-start.5 = (f32[8,4096]{1,0:T(8,128)}, f32[8,4096]{1,0:T(8,128)S(1)}, u32[]{:S(2)}) copy-start(f32[8,4096]{1,0:T(8,128)S(1)} %get-tuple-element.37.lse_all) | copy-start | bytes 393220
  110.7 6.0 %copy-start.14 = (bf16[1,256,1024]{2,1,0:T(8,128)(2,1)S(1)}, bf16[1,256,1024]{2,1,0:T(8,128)(2,1)}, u32[]{:S(2)}) copy-start(bf16[1,256,1024]{2,1,0:T(8,128)(2,1)} %param.20) | copy-start | bytes 1572868
  116.6 25.2 %copy-start.25 = (f32[256,4096]{1,0:T(8,128)}, f32[256,4096]{1,0:T(8,128)S(1)}, u32[]{:S(2)}) copy-start(f32[256,4096]{1,0:T(8,128)S(1)} %convolution_add_fusion) | copy-start | bytes 12582916
  132.4 9.4 %copy-start.6 = (f32[256,1024]{1,0:T(8,128)}, f32[256,1024]{1,0:T(8,128)S(1)}, u32[]{:S(2)}) copy-start(f32[256,1024]{1,0:T(8,128)S(1)} %get-tuple-element.56) | copy-start | bytes 3145732
  289.6 2.7 copy-start.10
  289.6 4.5 %copy-start.8 = (bf16[1,256,1024]{2,1,0:T(8,128)(2,1)S(1)}, bf16[1,256,1024]{2,1,0:T(8,128)(2,1)}, u32[]{:S(2)}) copy-start(bf16[1,256,1024]{2,1,0:T(8,128)(2,1)} %param.18) | copy-start | bytes 1572868
  289.6 4.5 %copy-start.13 = (bf16[1024,256]{1,0:T(8,128)(2,1)S(1)}, bf16[1024,256]{1,0:T(8,128)(2,1)}, u32[]{:S(2)}) copy-start(bf16[1024,256]{1,0:T(8,128)(2,1)} %get-tuple-element.40) | copy-start | bytes 1572868
  289.6 4.6 %copy-start.19 = (f32[1024]{0:T(1024)S(1)}, f32[1024]{0:T(1024)}, u32[]{:S(2)}) copy-start(f32[1024]{0:T(1024)} %param.32) | copy-start | bytes 12292
  294.2 6.1 %copy-start.23 = (f32[1024]{0:T(1024)S(1)}, f32[1024]{0:T(1024)}, u32[]{:S(2)}) copy-start(f32[1024]{0:T(1024)} %param.31) | copy-start | bytes 12292
  361.0 7.5 %copy-start.15 = (f32[32,1024]{1,0:T(8,128)S(1)}, f32[32,1024]{1,0:T(8,128)}, u32[]{:S(2)}) copy-start(f32[32,1024]{1,0:T(8,128)} %get-tuple-element.99) | copy-start | bytes 393220
  364.7 6.3 %copy-start.12 = (f32[128,1024]{1,0:T(8,128)S(1)}, f32[128,1024]{1,0:T(8,128)}, u32[]{:S(2)}) copy-start(f32[128,1024]{1,0:T(8,128)} %get-tuple-element.101) | copy-start | bytes 1572868
Sparse Core Ops, SparseCore 0:
  12.2 111.8 all-gather.1

commit v3 on v2

--- a/solution.py
+++ b/solution.py
@@ -243,10 +243,10 @@
 
 CHUNKS = 9
 TICKS = CHUNKS + 4
-
-
-def halving_plan(sources, own, got0, got1a, got1b, got2, got3, got4, total, sems):
-    load_sem, send_sem, recv_sem = sems
+SLOTS = 3
+
+
+def halving_plan(full, got0, got1a, got1b, got2a, got2b, got3, got4, total, send_sem, recv_sem):
     me = lax.axis_index("seq")
     x = lax.axis_index("scene")
     core = lax.rem(me, 2)
@@ -258,177 +258,209 @@
     at_y = (x, me + 2 - 4 * y)
     at_z0 = (x, me + 4 - 8 * z0)
     at_z1 = (x, me + 8 - 16 * z1)
-    top, low = slice(0, 16), slice(16, 32)
+    up, low = slice(0, 64), slice(64, 128)
 
     def copy_of(slot, c):
         src, dst, device = (
-            lambda: (got0.at[c], got0.at[c], at_core),
-            lambda: (own.at[c, 1 - x, :, :, top, :], got1a.at[c], at_x),
-            lambda: (own.at[c, :, :, 1 - y, low, :], got1b.at[c], at_y),
-            lambda: (got1a.at[c, :, 1 - y], got2.at[c, :, top, :], at_y),
-            lambda: (got1b.at[c, 1 - x], got2.at[c, :, low, :], at_x),
-            lambda: (got2.at[c, 1 - z0], got3.at[c, 0], at_z0),
-            lambda: (got2.at[c, 3 - z0], got3.at[c, 1], at_z0),
+            lambda: (full.at[lax.rem(c, SLOTS), :, :, :, :, 1 - core], got0.at[c], at_core),
+            lambda: (got0.at[c, 1 - x, :, :, :, up, :], got1a.at[c], at_x),
+            lambda: (got0.at[c, :, :, :, 1 - y, low, :], got1b.at[c], at_y),
+            lambda: (got1a.at[c, :, 1 - z0], got2a.at[c], at_z0),
+            lambda: (got1b.at[c, 1 - x], got2b.at[c], at_x),
+            lambda: (got2a.at[c, :, 1 - y], got3.at[c, :, up, :], at_y),
+            lambda: (got2b.at[c, :, 1 - z0], got3.at[c, :, low, :], at_z0),
             lambda: (got3.at[c, 1 - z1], got4.at[c], at_z1),
         )[slot]()
         return remote(src, dst, send_sem.at[c, slot], recv_sem.at[c, slot], device)
 
-    def first_copies(c):
-        ref, rows, columns = sources[c]
-        load = pltpu.make_async_copy(
-            ref.at[:, :, :, core, rows, columns], own.at[c], load_sem.at[c]
-        )
-        over = remote(
-            ref.at[:, :, :, 1 - core, rows, columns],
-            got0.at[c],
-            send_sem.at[c, 0],
-            recv_sem.at[c, 0],
-            at_core,
-        )
-        return load, over
-
-    def begin():
-        for c in range(CHUNKS):
-            for copy in first_copies(c):
-                copy.start()
-
-    def stage1(c):
-        pltpu.make_async_copy(own.at[c], own.at[c], load_sem.at[c]).wait()
+    def sum1(c):
         copy_of(0, c).wait_recv()
-        own[c] = own[c] + got0[c]
+        got0[c] = got0[c] + full[lax.rem(c, SLOTS), :, :, :, :, core]
+
+    def start1(c):
         copy_of(1, c).start()
         copy_of(2, c).start()
 
     def stage2(c):
         copy_of(1, c).wait_recv()
-        got1a[c] = own[c, x, :, :, top, :] + got1a[c]
+        got1a[c] = got1a[c] + got0[c, x, :, :, :, up, :]
         copy_of(3, c).start()
         copy_of(2, c).wait_recv()
-        got1b[c] = own[c, :, :, y, low, :] + got1b[c]
+        got1b[c] = got1b[c] + got0[c, :, :, :, y, low, :]
         copy_of(4, c).start()
 
     def stage3(c):
         copy_of(3, c).wait_recv()
-        got2[c, :, top, :] = got1a[c, :, y] + got2[c, :, top, :]
+        got2a[c] = got2a[c] + got1a[c, :, z0]
+        copy_of(5, c).start()
         copy_of(4, c).wait_recv()
-        got2[c, :, low, :] = got1b[c, x] + got2[c, :, low, :]
-        copy_of(5, c).start()
+        got2b[c] = got2b[c] + got1b[c, x]
         copy_of(6, c).start()
 
     def stage4(c):
         copy_of(5, c).wait_recv()
+        got3[c, :, up, :] = got3[c, :, up, :] + got2a[c, :, y]
         copy_of(6, c).wait_recv()
-        got3[c, 0] = got2[c, z0] + got3[c, 0]
-        got3[c, 1] = got2[c, 2 + z0] + got3[c, 1]
+        got3[c, :, low, :] = got3[c, :, low, :] + got2b[c, :, z0]
         copy_of(7, c).start()
 
     def stage5(c):
         copy_of(7, c).wait_recv()
         total[c] = got3[c, z1].astype(f32) + got4[c].astype(f32)
 
-    stages = (stage1, stage2, stage3, stage4, stage5)
-
     def tick(when):
-        for depth in reversed(range(len(stages))):
-            c = when - depth
+        for stage, c in (
+            (stage5, when - 4),
+            (stage4, when - 3),
+            (stage3, when - 2),
+            (stage2, when - 1),
+            (start1, when + 1),
+        ):
 
             @pl.when((c >= 0) & (c < CHUNKS))
-            def _(stage=stages[depth], c=c):
+            def _(stage=stage, c=c):
                 stage(c)
 
-    def finish(sinks):
-        for c, (ref, rows, columns) in enumerate(sinks):
-            pltpu.make_async_copy(total.at[c], ref.at[rows, columns], load_sem.at[c]).start()
-        for c in range(CHUNKS):
-            for slot in range(8):
-                copy_of(slot, c).wait_send()
-        for c, (ref, rows, columns) in enumerate(sinks):
-            pltpu.make_async_copy(total.at[c], ref.at[rows, columns], load_sem.at[c]).wait()
-
-    return [at_core, at_x, at_y, at_z0, at_z1], begin, tick, finish
-
-
-def halving_pieces(down, up, out):
-    every = slice(None)
-    return (
-        [(down, slice(32 * i, 32 * i + 32), every) for i in range(4)]
-        + [(up, every, slice(1024 * i, 1024 * i + 1024)) for i in range(4)]
-        + [(out, every, every)]
-    )
-
-
-def halving_scratch():
-    dma = pltpu.SemaphoreType.DMA
-    return [
-        pltpu.VMEM((CHUNKS, 2, 4, 2, 32, 1024), bf16),
-        pltpu.VMEM((CHUNKS, 2, 4, 2, 32, 1024), bf16),
-        pltpu.VMEM((CHUNKS, 4, 2, 16, 1024), bf16),
-        pltpu.VMEM((CHUNKS, 2, 4, 16, 1024), bf16),
-        pltpu.VMEM((CHUNKS, 4, 32, 1024), bf16),
-        pltpu.VMEM((CHUNKS, 2, 32, 1024), bf16),
-        pltpu.VMEM((CHUNKS, 32, 1024), bf16),
-        pltpu.VMEM((CHUNKS, 32, 1024), f32),
-        dma((CHUNKS,)),
-        dma((CHUNKS, 8)),
-        dma((CHUNKS, 8)),
-    ]
-
-
-def backward_kernel(
-    n,
-    tok,
-    dt_ref,
-    q_all,
-    k_all,
-    v_all,
-    o_all,
-    lse_all,
-    down_ref,
-    up_ref,
-    out_ref,
-    dq_ref,
-    dk_ref,
-    dv_ref,
-    heads_ref,
-    down_sum,
-    up_sum,
-    out_sum,
-    d_all,
-    q_nat,
-    k_nat,
-    v_nat,
-    d_nat,
-    delta,
-    dq_acc,
-    low,
-    in_send,
-    in_recv,
-    in_local,
-    kv_send,
-    kv_recv,
-    kv_local,
-    q_send,
-    q_recv,
-    q_local,
-    save_sem,
-    *halving,
-):
+    return copy_of, sum1, start1, tick
+
+
+def tail_kernel(n, tok, *refs):
+    (
+        dt_ref,
+        q_ref,
+        k_ref,
+        v_ref,
+        o_ref,
+        lse_ref,
+        act_ref,
+        masked_ref,
+        two_ref,
+        hidden_ref,
+        att_ref,
+        low_ref,
+        normed_ref,
+        wq_ref,
+        wk_ref,
+        wv_ref,
+        tokens_ref,
+        resid_ref,
+        gain_ref,
+        early_ref,
+        early_up_ref,
+        tokens_out,
+        total,
+        pack_got,
+        small_got,
+        small_up_got,
+        q_all,
+        k_all,
+        v_all,
+        d_all,
+        q_nat,
+        k_nat,
+        v_nat,
+        d_nat,
+        o_all,
+        lse_all,
+        delta,
+        dq_acc,
+        low,
+        act,
+        masked,
+        two,
+        hidden,
+        att,
+        resid_low,
+        act_t,
+        two_t,
+        full,
+        got0,
+        got1a,
+        got1b,
+        got2a,
+        got2b,
+        got3,
+        got4,
+        land,
+        back_in,
+        rows_in,
+        resid,
+        pack,
+        small,
+        small_up,
+        load_sem,
+        weight_sem,
+        normed_sem,
+        in_send,
+        in_recv,
+        in_local,
+        kv_send,
+        kv_recv,
+        kv_local,
+        q_send,
+        q_recv,
+        q_local,
+        half_send,
+        half_recv,
+        pack_send,
+        pack_recv,
+        small_send,
+        small_recv,
+        small_up_send,
+        small_up_recv,
+        last_local,
+    ) = refs
     me = lax.axis_index("seq")
     scene = lax.axis_index("scene")
     chip, core = me // 2, lax.rem(me, 2)
     chips = n // 2
     length = n * tok
     wide = 2 * tok
-    partners, begin, tick, finish = halving_plan(
-        halving_pieces(down_ref, up_ref, out_ref), *halving[:8], halving[8:]
-    )
-    greet([(scene, lax.rem(me + j, n)) for j in range(1, n)] + [partners[1]])
+    devices = 2 * n
+    width = masked.shape[1]
+    mine = scene * n + me
 
     def rows(head):
         return pl.ds(pl.multiple_of(head * HEAD_DIM, HEAD_DIM), HEAD_DIM)
 
     def lanes(block, width=tok):
         return pl.ds(pl.multiple_of(block * width, width), width)
+
+    def by_block(ref, block):
+        return ref.at[:, 1024 * block : 1024 * block + 1024]
+
+    loads = [
+        pltpu.make_async_copy(src, dst, load_sem.at[i])
+        for i, (src, dst) in enumerate(
+            [(by_block(act_ref, i), act.at[tok * i : tok * i + tok, :]) for i in range(4)]
+            + [
+                (masked_ref, masked),
+                (q_ref, q_all),
+                (k_ref, k_all),
+                (v_ref, v_all),
+                (o_ref, o_all),
+                (lse_ref, lse_all),
+                (two_ref, two),
+            ]
+            + [(by_block(hidden_ref, i), hidden.at[tok * i : tok * i + tok, :]) for i in range(4)]
+            + [
+                (att_ref, att),
+                (low_ref, resid_low),
+                (early_ref, small.at[4:8]),
+                (early_up_ref, small_up),
+                (tokens_ref, rows_in),
+                (resid_ref, resid),
+            ]
+        )
+    ]
+    for load in loads:
+        load.start()
+
+    def peer(j):
+        index = lax.rem(mine + j, devices)
+        return index, (index // n, lax.rem(index, n))
+
+    greet([peer(j)[1] for j in range(1, devices)])
 
     copies = []
     for j in range(1, n):
@@ -445,11 +477,100 @@
         copies[-1].start()
     local = pltpu.make_async_copy(dt_ref.at[rows(me), :], d_all.at[:, lanes(me)], in_local)
     local.start()
-    begin()
+
+    half, sum1, start1, tick = halving_plan(
+        full, got0, got1a, got1b, got2a, got2b, got3, got4, total, half_send, half_recv
+    )
+
+    def chunk_begin(c):
+        @pl.when(c >= SLOTS)
+        def _():
+            half(0, c - SLOTS).wait_send()
+
+        return lax.rem(c, SLOTS)
+
+    def chunk_end(c):
+        half(0, c).start()
+
+        @pl.when(c >= 1)
+        def _():
+            sum1(c - 1)
+
+    def down_chunk(c):
+        slot = chunk_begin(c)
+        columns = masked[:, lanes(c, 256)]
+        for block in range(4):
+            part = contract(act_t[1024 * block : 1024 * block + 1024, :], columns, 1, 0)
+            full[slot, block // 2, block % 2] = part.astype(bf16).reshape(2, 2, 2, 128, 256)
+        chunk_end(c)
+
+    def narrow_chunk(c, left, right):
+        slot = chunk_begin(c)
+        for block in range(4):
+            part = contract(left, right[:, 256 * block : 256 * block + 256], 1, 0)
+            full[slot, :, :, :, :, :, 32 * block : 32 * block + 32, :] = part.astype(bf16).reshape(
+                2, 2, 2, 2, 2, 32, 256
+            )
+        chunk_end(c)
+
+    for block in range(4):
+        loads[block].wait()
+        act_t[1024 * block : 1024 * block + 1024, :] = act[tok * block : tok * block + tok, :].T
+    loads[4].wait()
+
+    def first_chunk(c, carry):
+        down_chunk(c)
+
+        @pl.when(c >= 1)
+        def _():
+            start1(c - 1)
+
+        return carry
+
+    lax.fori_loop(0, 3, first_chunk, 0)
+    for load in loads[5:11]:
+        load.wait()
+    two_t[...] = two[...].T
     q_nat[...] = q_all[...].T
     k_nat[...] = k_all[...].T
     v_nat[...] = v_all[...].T
     dq_acc[...] = jnp.zeros_like(dq_acc)
+    for load in loads[11:17]:
+        load.wait()
+
+    def chunk(step):
+        @pl.when(step == 0)
+        def _():
+            down_chunk(step + 3)
+
+        @pl.when((step >= 1) & (step < 5))
+        def _():
+            there = pl.ds(pl.multiple_of((step - 1) * tok, tok), tok)
+            narrow_chunk(step + 3, two_t[...], hidden[there, :])
+
+        @pl.when(step == 5)
+        def _():
+            narrow_chunk(step + 3, att[...], resid_low[...])
+
+        @pl.when(step == 6)
+        def _():
+            sum1(CHUNKS - 1)
+
+        @pl.when(step == 1)
+        def _():
+            normed_load(0).start()
+
+        @pl.when(step == 5)
+        def _():
+            normed_load(1).start()
+
+    def normed_load(i):
+        return pltpu.make_async_copy(
+            normed_ref.at[1024 * i : 1024 * i + 1024, :],
+            (act, hidden)[i % 2],
+            normed_sem.at[i % 2],
+        )
+
     local.wait()
     for copy in copies:
         copy.wait_recv()
@@ -463,7 +584,7 @@
         device = 2 * target + lax.rem(core + flip, 2)
         return remote(
             low.at[0, :, lanes(device)],
-            dq_ref.at[rows(me), :],
+            land.at[0, rows(me), :],
             q_send.at[step, flip],
             q_recv.at[step, flip],
             (scene, device),
@@ -474,16 +595,15 @@
         device = 2 * target + lax.rem(core + flip, 2)
         return remote(
             low.at[1 + a, :, lanes(device)],
-            (dk_ref, dv_ref)[a].at[rows(me), :],
+            land.at[1 + a, rows(me), :],
             kv_send.at[a, step, flip],
             kv_recv.at[a, step, flip],
             (scene, device),
         )
 
-    mine = [
-        pltpu.make_async_copy(low.at[0, :, lanes(me)], dq_ref.at[rows(me), :], q_local),
-        pltpu.make_async_copy(low.at[1, :, lanes(me)], dk_ref.at[rows(me), :], kv_local.at[0]),
-        pltpu.make_async_copy(low.at[2, :, lanes(me)], dv_ref.at[rows(me), :], kv_local.at[1]),
+    own = [
+        pltpu.make_async_copy(low.at[a, :, lanes(me)], land.at[a, rows(me), :], sem)
+        for a, sem in ((0, q_local), (1, kv_local.at[0]), (2, kv_local.at[1]))
     ]
 
     def keys(step, last):
@@ -509,7 +629,7 @@
             if last:
                 low[0, :, there] = (dq * score_scale).astype(bf16)
                 if i == 0:
-                    mine[0].start()
+                    own[0].start()
                 else:
                     q_copy(i, 0).start()
                 q_copy(i, 1).start()
@@ -518,75 +638,218 @@
         low[1, :, span] = dk.astype(bf16).T
         low[2, :, span] = dv.astype(bf16).T
 
-    tick(0)
-    keys(0, False)
-    mine[1].start()
-    mine[2].start()
-    kv_copy(0, 0, 1).start()
-    kv_copy(1, 0, 1).start()
-
-    def send_kv(step):
+    def step_body(step, carry):
+        chunk(step)
+        tick(step + 1)
+        keys(step, False)
+
+        @pl.when(step == 0)
+        def _():
+            own[1].start()
+            own[2].start()
+
         for a in range(2):
-            kv_copy(a, step, 0).start()
+
+            @pl.when(step > 0)
+            def _(a=a):
+                kv_copy(a, step, 0).start()
+
             kv_copy(a, step, 1).start()
-
-    def step_body(step, carry):
-        tick(step)
-        keys(step, False)
-        send_kv(step)
         return carry
 
-    lax.fori_loop(1, chips - 1, step_body, 0)
-    tick(chips - 1)
+    lax.fori_loop(0, chips - 1, step_body, 0)
+    for c in range(CHUNKS - SLOTS, CHUNKS):
+        half(0, c).wait_send()
+    weight_loads = []
+    for a, ref in enumerate((wq_ref, wk_ref, wv_ref)):
+        for block in range(4):
+            weight_loads.append(
+                pltpu.make_async_copy(
+                    ref.at[:, :, :, :, 256 * block : 256 * block + 256],
+                    full.at[a, block // 2, block % 2],
+                    weight_sem.at[a, block],
+                )
+            )
+            weight_loads[-1].start()
+    tick(8)
     keys(chips - 1, True)
-    send_kv(chips - 1)
-    save = pltpu.make_async_copy(low, heads_ref, save_sem)
-    save.start()
-
-    def tick_body(when, carry):
-        tick(when)
+    for a in range(2):
+        kv_copy(a, chips - 1, 0).start()
+        kv_copy(a, chips - 1, 1).start()
+    tick(9)
+
+    head_acc = None
+    for i in range(length // 1024):
+        normed_load(i).wait()
+        left = low[:, :, 1024 * i : 1024 * i + 1024].reshape(3 * HEAD_DIM, 1024)
+        part = contract(left, (act, hidden)[i % 2][...], 1, 0)
+        head_acc = part if head_acc is None else head_acc + part
+        if i + 2 < length // 1024:
+            normed_load(i + 2).start()
+    tick(10)
+    by_row = head_acc.T
+    share = width // devices
+    pack[:, :share, :] = by_row[:, : 2 * HEAD_DIM].astype(bf16).reshape(devices, share, 2 * HEAD_DIM)
+    third = by_row[:, 2 * HEAD_DIM :].astype(bf16).reshape(devices, 2, share // 2, HEAD_DIM)
+    pack[:, share:, :] = jnp.concatenate([third[:, 0], third[:, 1]], axis=-1)
+
+    def pack_copy(j):
+        index, device = peer(j)
+        return remote(
+            pack.at[index], pack_got.at[mine], pack_send.at[j], pack_recv.at[j], device
+        )
+
+    def small_copy(j):
+        index, device = peer(j)
+        return remote(
+            small.at[:, lanes(index // 4, 128)],
+            small_got.at[mine],
+            small_send.at[j],
+            small_recv.at[j],
+            device,
+        )
+
+    def small_up_copy(j):
+        index, device = peer(j)
+        return remote(
+            small_up.at[index], small_up_got.at[mine], small_up_send.at[j], small_up_recv.at[j], device
+        )
+
+    kept = [
+        pltpu.make_async_copy(pack.at[mine], pack_got.at[mine], last_local.at[0]),
+        pltpu.make_async_copy(
+            small.at[:, lanes(mine // 4, 128)], small_got.at[mine], last_local.at[1]
+        ),
+        pltpu.make_async_copy(small_up.at[mine], small_up_got.at[mine], last_local.at[2]),
+    ]
+    loads[17].wait()
+    loads[18].wait()
+    kept[0].start()
+    kept[2].start()
+
+    def pack_body(j, carry):
+        pack_copy(j).start()
+        small_up_copy(j).start()
         return carry
 
-    lax.fori_loop(chips, TICKS, tick_body, 0)
-    finish(halving_pieces(down_sum, up_sum, out_sum))
-    for copy in copies:
-        copy.wait_send()
-    for copy in mine:
+    lax.fori_loop(1, devices, pack_body, 0)
+    tick(11)
+
+    for copy in own:
         copy.wait()
     for step in range(chips):
         for flip in range(2):
-            if step == 0 and flip == 0:
-                continue
-            kv_copy(0, step, flip).wait()
-            kv_copy(1, step, flip).wait()
-            q_copy(step, flip).wait()
-    save.wait()
-
-
-def attention_backward(n, d_t, q_all, k_all, v_all, o_all, lse_all, *weights):
-    shards = 32
-    tok = d_t.shape[1]
+            if step or flip:
+                kv_copy(0, step, flip).wait_recv()
+                kv_copy(1, step, flip).wait_recv()
+                q_copy(step, flip).wait_recv()
+    for load in loads[19:] + weight_loads:
+        load.wait()
+    for i in range(4):
+        part = None
+        for a in range(3):
+            left = jnp.concatenate(
+                [full[a, b // 2, b % 2, i // 2, i % 2].reshape(256, 256) for b in range(4)], axis=1
+            )
+            here = contract(left, land[a], 1, 0)
+            part = here if part is None else part + here
+        back_in[:, 256 * i : 256 * i + 256] = part.T
+    back = back_in[...]
+    scaled, inverse = normalise(rows_in[...].astype(f32))
+    token_part, gain_grad, shift_grad = norm_back(back, scaled, inverse, gain_ref[...])
+    tokens_out[...] = (resid[...] + token_part).astype(bf16)
+    ones = jnp.ones((8, tok), bf16)
+    small[0:1, :] = contract(ones, land[0], 1, 1)[0:1]
+    small[1:2, :] = contract(ones, land[2], 1, 1)[0:1]
+    small[2:3, :] = gain_grad[None]
+    small[3:4, :] = shift_grad[None]
+    kept[1].start()
+
+    def small_body(j, carry):
+        small_copy(j).start()
+        return carry
+
+    lax.fori_loop(1, devices, small_body, 0)
+
+    tick(12)
+    for copy in kept:
+        copy.wait()
+
+    def arrive(j, carry):
+        pack_copy(j).wait()
+        small_up_copy(j).wait()
+        small_copy(j).wait()
+        return carry
+
+    lax.fori_loop(1, devices, arrive, 0)
+    for copy in copies:
+        copy.wait_send()
+    for step in range(chips):
+        for flip in range(2):
+            if step or flip:
+                kv_copy(0, step, flip).wait_send()
+                kv_copy(1, step, flip).wait_send()
+                q_copy(step, flip).wait_send()
+
+    def settle(c, carry):
+        for slot in range(1, 8):
+            half(slot, c).wait_send()
+        return carry
+
+    lax.fori_loop(0, CHUNKS, settle, 0)
+
+
+def tail(n, tok, width, hidden_width, *arrays):
     length = n * tok
     chips = n // 2
+    devices = 2 * n
+    share = width // devices
     any_spec = pl.BlockSpec(memory_space=pl.ANY)
     vmem = pl.BlockSpec(memory_space=pltpu.VMEM)
     dma = pltpu.SemaphoreType.DMA
-    part = jax.ShapeDtypeStruct(d_t.shape, bf16)
-    return pl.pallas_call(
-        functools.partial(backward_kernel, n, tok),
-        out_shape=(part, part, part, jax.ShapeDtypeStruct((3, HEAD_DIM, length), bf16))
-        + tuple(jax.ShapeDtypeStruct((w.shape[0] // shards, w.shape[1]), f32) for w in weights),
-        in_specs=[any_spec] + [vmem] * 5 + [any_spec] * 3,
-        out_specs=[any_spec] * 7,
-        scratch_shapes=[
-            pltpu.VMEM((HEAD_DIM, length), bf16),
-            pltpu.VMEM((length, HEAD_DIM), bf16),
-            pltpu.VMEM((length, HEAD_DIM), bf16),
-            pltpu.VMEM((length, HEAD_DIM), bf16),
-            pltpu.VMEM((length, HEAD_DIM), bf16),
-            pltpu.VMEM((8, length), f32),
-            pltpu.VMEM((HEAD_DIM, length), f32),
-            pltpu.VMEM((3, HEAD_DIM, length), bf16),
+
+    def space(*shape, kind=bf16):
+        return pltpu.VMEM(shape, kind)
+
+    def out(*shape, kind=f32):
+        return jax.ShapeDtypeStruct(shape, kind)
+
+    pieces = CHUNKS
+    scratch = (
+        [space(HEAD_DIM, length)] * 4
+        + [space(length, HEAD_DIM)] * 4
+        + [
+            space(HEAD_DIM, length, kind=f32),
+            space(8, length, kind=f32),
+            space(8, length, kind=f32),
+            space(HEAD_DIM, length, kind=f32),
+            space(3, HEAD_DIM, length),
+            space(hidden_width // 1024 * tok, 1024),
+            space(tok, width),
+            space(tok, width),
+            space(hidden_width // 1024 * tok, 1024),
+            space(width, tok),
+            space(tok, width),
+            space(hidden_width, tok),
+            space(width, tok),
+            space(SLOTS, 2, 2, 2, 2, 2, 128, 256),
+            space(pieces, 2, 2, 2, 2, 128, 256),
+            space(pieces, 2, 2, 2, 64, 256),
+            space(pieces, 2, 2, 2, 64, 256),
+            space(pieces, 2, 2, 64, 256),
+            space(pieces, 2, 2, 64, 256),
+            space(pieces, 2, 128, 256),
+            space(pieces, 128, 256),
+            space(3, width, tok),
+            space(tok, width, kind=f32),
+            space(tok, width),
+            space(tok, width, kind=f32),
+            space(devices, share + share // 2, 128),
+            space(8, width, kind=f32),
+            space(devices, 8, 128, kind=f32),
+            dma((21,)),
+            dma((3, 4)),
+            dma((2,)),
             dma((n,)),
             dma((n,)),
             dma,
@@ -596,73 +859,94 @@
             dma((chips, 2)),
             dma((chips, 2)),
             dma,
-            dma,
+            dma((pieces, 8)),
+            dma((pieces, 8)),
         ]
-        + halving_scratch(),
+        + [dma((devices,))] * 6
+        + [dma((3,))]
+    )
+    in_specs = [any_spec] * 21
+    in_specs[18] = vmem
+    return pl.pallas_call(
+        functools.partial(tail_kernel, n, tok),
+        out_shape=(
+            out(tok, width, kind=bf16),
+            out(pieces, 128, 256),
+            out(devices, share + share // 2, 128, kind=bf16),
+            out(devices, 8, 128),
+            out(devices, 8, 128),
+        ),
+        in_specs=in_specs,
+        out_specs=[vmem] * 5,
+        scratch_shapes=scratch,
         compiler_params=pltpu.CompilerParams(
-            collective_id=1, has_side_effects=True, vmem_limit_bytes=60 << 20
+            collective_id=1, has_side_effects=True, vmem_limit_bytes=63 << 20
         ),
-        name="attention_backward",
-    )(
-        d_t,
-        q_all,
-        k_all,
-        v_all,
-        o_all,
-        lse_all,
-        *(w.reshape(2, 4, 2, 2, w.shape[0] // shards, w.shape[1]) for w in weights),
-    )
-
-
-def exchange_kernel(scenes, n, count, *refs):
-    sources, sinks = refs[:count], refs[count : 2 * count]
-    send_sem, recv_sem, local_sem = refs[2 * count :]
-    me = lax.axis_index("seq")
-    scene = lax.axis_index("scene")
-    mine = scene * n + me
-    devices = scenes * n
-
-    def peer(j):
-        index = lax.rem(mine + j, devices)
-        return index, (index // n, lax.rem(index, n))
-
-    greet([peer(j)[1] for j in range(1, devices)])
-    copies = []
-    for a in range(count):
-        copies.append(
-            pltpu.make_async_copy(sources[a].at[mine], sinks[a].at[mine], local_sem.at[a])
-        )
-        copies[-1].start()
-    for j in range(1, devices):
-        index, device = peer(j)
-        for a in range(count):
-            copies.append(
-                remote(
-                    sources[a].at[index],
-                    sinks[a].at[mine],
-                    send_sem.at[a, j],
-                    recv_sem.at[a, j],
-                    device,
-                )
+        name="tail",
+    )(*arrays)
+
+
+def finish_kernel(n, *refs):
+    tokens_in, total, pack_got, small_got, small_up_got, tokens_out = refs[:6]
+    query_out, key_out, value_out, out_out, up_out, down_out = refs[6:12]
+    vectors, up_vector = refs[12:20], refs[20]
+    tokens_out[...] = tokens_in[...]
+    mine = lax.axis_index("scene") * n + lax.axis_index("seq")
+    share = query_out.shape[0]
+    for head in range(0, n, 2):
+        pair = [
+            pack_got[head + i].astype(f32) + pack_got[n + head + i].astype(f32) for i in range(2)
+        ]
+        columns = slice(head * HEAD_DIM, head * HEAD_DIM + 2 * HEAD_DIM)
+
+        def joined(first, last, start):
+            return jnp.concatenate(
+                [part[first:last, start : start + HEAD_DIM] for part in pair], axis=1
             )
-            copies[-1].start()
-    for copy in copies:
-        copy.wait()
-
-
-def exchange(scenes, n, *arrays):
-    any_spec = pl.BlockSpec(memory_space=pl.ANY)
-    dma = pltpu.SemaphoreType.DMA
-    count, devices = len(arrays), scenes * n
+
+        query_out[:, columns] = joined(0, share, 0)
+        key_out[:, columns] = joined(0, share, HEAD_DIM)
+        value_out[: share // 2, columns] = joined(share, share + share // 2, 0)
+        value_out[share // 2 :, columns] = joined(share, share + share // 2, HEAD_DIM)
+    for i in range(4):
+        down_out[:, 256 * i : 256 * i + 256] = total[i]
+        out_out[:, 256 * i : 256 * i + 256] = total[8, 32 * i : 32 * i + 32, :]
+    for i in range(16):
+        up_out[:, 256 * i : 256 * i + 256] = total[4 + i // 4, 32 * (i % 4) : 32 * (i % 4) + 32, :]
+    turn = lax.rem(128 - 32 * lax.rem(mine, 4), 128)
+    sums = pltpu.roll(jnp.sum(small_got[...], axis=0), turn, 1)
+    for i, vector in enumerate(vectors):
+        vector[...] = sums[i, :share]
+    up_vector[...] = jnp.sum(small_up_got[...], axis=0)[0]
+
+
+def finish(n, tokens_grad, total, pack_got, small_got, small_up_got):
+    tok, width = tokens_grad.shape
+    devices = 2 * n
+    share = width // devices
+    vmem = pl.BlockSpec(memory_space=pltpu.VMEM)
+
+    def out(*shape):
+        return jax.ShapeDtypeStruct(shape, f32)
+
     return pl.pallas_call(
-        functools.partial(exchange_kernel, scenes, n, count),
-        out_shape=tuple(jax.ShapeDtypeStruct(a.shape, a.dtype) for a in arrays),
-        in_specs=[any_spec] * count,
-        out_specs=[any_spec] * count,
-        scratch_shapes=[dma((count, devices)), dma((count, devices)), dma((count,))],
-        compiler_params=pltpu.CompilerParams(collective_id=3, has_side_effects=True),
-        name="exchange",
-    )(*arrays)
+        functools.partial(finish_kernel, n),
+        out_shape=(
+            jax.ShapeDtypeStruct((tok, width), bf16),
+            out(share, width),
+            out(share, width),
+            out(share, width),
+            out(share, width),
+            out(share, 4 * width),
+            out(4 * share, width),
+        )
+        + (out(share),) * 8
+        + (out(4 * share),),
+        in_specs=[vmem] * 5,
+        out_specs=[vmem] * 16,
+        compiler_params=pltpu.CompilerParams(vmem_limit_bytes=60 << 20),
+        name="finish",
+    )(tokens_grad, total, pack_got, small_got, small_up_got)
 
 
 def normalise(values):
@@ -733,10 +1017,8 @@
     activated = activated.astype(bf16)
     block_out = (residual + matmul(activated, w_down) + b_down).astype(bf16)
     masked = out_grad[0] * surface_mask[0].astype(bf16)[:, None]
-    grad_down = matmul_tn(activated, masked).astype(bf16)
     grad_bdown = jnp.sum(masked.astype(f32), axis=0)
     hidden_grad = (matmul_nt(masked, w_down) * gelu_grad).astype(bf16)
-    grad_up = matmul_tn(normed_two, hidden_grad).astype(bf16)
     grad_bup = jnp.sum(hidden_grad.astype(f32), axis=0)
     norm_two_in = matmul_nt(hidden_grad, w_up)
     resid_part, grad_gain_two, grad_shift_two = norm_back(
@@ -744,58 +1026,42 @@
     )
     resid_grad = masked.astype(f32) + resid_part
     resid_low = resid_grad.astype(bf16)
-    grad_out = matmul(att_t, resid_low).astype(bf16)
     grad_bout = jnp.sum(resid_low.astype(f32), axis=0)
     att_grad_t = matmul_nt(w_out, resid_low).astype(bf16)
 
-    dq_t, dk_t, dv_t, heads_t, sum_down, sum_up, sum_out = attention_backward(
-        n, att_grad_t, q_all, k_all, v_all, o_all, lse_all, grad_down, grad_up, grad_out
-    )
-
-    head_grads = matmul(heads_t.reshape(3 * HEAD_DIM, n * tok), normed_all)
-    head_grads = head_grads.T.reshape(devices, width // devices, 3 * HEAD_DIM)
-    norm_one_in = (
-        contract(dq_t, w_query, 0, 1) + contract(dk_t, w_key, 0, 1) + contract(dv_t, w_value, 0, 1)
-    )
-    token_part, grad_gain_one, grad_shift_one = norm_back(
-        norm_one_in, scaled_one, inverse_one, gain_one
-    )
-    tokens_grad = (resid_grad + token_part).astype(bf16)
-    grad_bquery = jnp.sum(dq_t.astype(f32), axis=1)
-    grad_bvalue = jnp.sum(dv_t.astype(f32), axis=1)
-    small = [
-        grad_bquery,
-        grad_bvalue,
-        grad_bout,
-        grad_bup,
-        grad_bdown,
-        grad_gain_one,
-        grad_shift_one,
-        grad_gain_two,
-        grad_shift_two,
-    ]
-    packed = jnp.concatenate([s.reshape(devices, -1) for s in small], axis=1)
-    room = -packed.shape[1] % 1024
-    packed = jnp.pad(packed, ((0, 0), (0, room))).reshape(devices, -1, 128)
-    heads_got, small_got = exchange(scenes, n, head_grads, packed)
-    heads_sum = heads_got.reshape(scenes, n, width // devices, 3, HEAD_DIM).sum(axis=0)
-    weights = [
-        jnp.moveaxis(heads_sum[:, :, i], 0, 1).reshape(width // devices, width) for i in range(3)
-    ]
-    vectors = small_got.reshape(devices, -1).sum(axis=0)
-    parts, at = [], 0
-    for s in small:
-        size = s.shape[0] // devices
-        parts.append(vectors[at : at + size])
-        at += size
-    bquery, bvalue, bout, bup, bdown, gone, sone, gtwo, stwo = parts
+    early = jnp.stack([grad_bout, grad_bdown, grad_gain_two, grad_shift_two])
+    early_up = jnp.broadcast_to(grad_bup.reshape(devices, 1, -1), (devices, 8, 128))
+    arrived = tail(
+        n,
+        tok,
+        width,
+        w_up.shape[1],
+        att_grad_t,
+        q_all,
+        k_all,
+        v_all,
+        o_all,
+        lse_all,
+        activated,
+        masked,
+        normed_two,
+        hidden_grad,
+        att_t,
+        resid_low,
+        normed_all,
+        *(w.reshape(2, 2, 2, 128, width) for w in (w_query, w_key, w_value)),
+        tokens[0],
+        resid_grad,
+        gain_one[None],
+        early,
+        early_up,
+    )
+    tokens_grad, *sums = finish(n, *arrived)
+    bquery, bvalue, gone, sone, bout, bdown, gtwo, stwo, bup = sums[6:]
     return (
         block_out[None],
         tokens_grad[None],
-        *weights,
-        sum_out,
-        sum_up,
-        sum_down,
+        *sums[:6],
         bquery,
         bvalue,
         bout,

time: 385 us -> 283 us (0.74)
  matrix products: 65.4 us -> 30 us
  Pallas kernels: 258 us -> 226 us
  local copies, waits for them, and re-layouts: 26.2 us -> 0.81 us
  other arithmetic: 14.5 us -> 7.66 us
    pallas_call x2, Pallas kernels: 168 us -> 140 us  [the longest x1 137 us: tail(): pl.pallas_call(functools.partial(tail_kernel, n, tok), out_shape=(out(tok...]
    dot_general x12 -> x7, matrix products: 42.1 us -> 23.3 us  [contract(): lax.dot_general(left, right, (((left_dim,), (right_dim,)), ((), ())), pre...]
    dot_general x4 -> x2, matrix products: 23.3 us -> 6.68 us  [matmul(): return jnp.dot(left, right, preferred_element_type=jnp.float32)]
    dot_general x1 -> x0, local copies, waits for them, and re-layouts: 11.7 us -> none  [matmul(): return jnp.dot(left, right, preferred_element_type=jnp.float32)]
    reshape x12 -> x0, local copies, waits for them, and re-layouts: 6.36 us -> none  [the longest x1 3.45 us: layer_on_device(): heads_got.reshape(scenes, n, width // devices, 3, HEAD_DIM).sum(axis=0)]
    reduce_sum x4 -> x1, other arithmetic: 5.95 us -> 0.19 us  [layer_on_device(): grad_bdown = jnp.sum(masked.astype(f32), axis=0)]
    pallas_call x1, Pallas kernels: 90.5 us -> 86.1 us  [attention_forward(): pl.pallas_call(functools.partial(forward_kernel, n, tok), out_shape=(jax....]
    unnamed x57 -> x56, local copies, waits for them, and re-layouts: 4.14 us -> 0.15 us
  transfers between devices with their start and end apart: 1 -> 1, of which waited for: 0 -> 0; matrix products, arithmetic and copies ran while one was open for 17% -> 12% of each run, Pallas kernels for 61% -> 31%
where the time goes in v3:
time: 283 us; the launch traced here: 279 us
  Pallas kernels  226 us (80%)
  matrix products  30 us (11%)
  between operations  14.8 us (5%)
  other arithmetic  7.66 us (3%)
    pallas_call x1, Pallas kernels, tail(): pl.pallas_call(functools.partial(tail_kernel, n, tok), out_shape=(out(tok...  137 us
    pallas_call x1, Pallas kernels, attention_forward(): pl.pallas_call(functools.partial(forward_kernel, n, tok), out_shape=(jax....  86.1 us
    dot_general x7, matrix products, contract(): lax.dot_general(left, right, (((left_dim,), (right_dim,)), ((), ())), pre...  23.3 us
    dot_general x2, matrix products, matmul(): return jnp.dot(left, right, preferred_element_type=jnp.float32)  6.68 us
  transfers between devices with their start and end apart: 1, of which 0 were waited for; matrix products, arithmetic and copies ran while one was open for 12% of the time, Pallas kernels for 31%

profile of v3, /device:TPU:0, one launch (start us, length us, event | category | flops | bytes accessed | tf_op | source)
XLA Modules:
  0.0 279.0 jit_solution(6973051689814704140)
XLA Ops:
  7.2 0.0 copy-start.8
  7.2 0.0 all-gather.2.cloned.1.call-start
  7.3 1.3 convert_reduce_fusion.1
  8.6 1.3 fusion.22
  9.9 2.1 fusion.25
  12.1 0.0 all-gather.2.cloned.1.call-update
  12.1 0.0 copy-start.9
  12.1 2.8 %fusion.18.kt_ref = bf16[1024,256]{1,0:T(8,128)(2,1)S(1)} fusion(bf16[256,1024]{1,0:T(8,128)(2,1)} %fusion.25, bf16[1024,1024]{1,0:T(8,128)(2,1)} %param.22), kind=kOutput, calls=%fused_computation.34 | convolution fusion | flops 537133056 | bytes 3145728 | tf_op jit(solution)/shard_map/dot_general | solution.py:26
  15.0 0.0 copy-start.25
  15.0 0.0 copy-start.6
  15.0 2.2 fusion.20.qt_ref
  17.2 1.0 fusion.17.vt_ref
  18.2 0.0 copy-start.16
  18.3 0.0 copy-start.20
  18.3 86.1 %attention_forward.1 = (bf16[1024,256]{1,0:T(8,128)(2,1)S(1)}, bf16[64,4096]{1,0:T(8,128)(2,1)S(1)}, bf16[64,4096]{1,0:T(8,128)(2,1)S(1)}, bf16[64,4096]{1,0:T(8...) custom-call(bf16[1024,256]{1,0:T(8,128)(2,1)S(1)} %fusion.20.qt_ref, bf16[1024,256]{1,0:T(8,128)(2,1)S(1)} %fusion.18.kt_ref, ...), custom_call_target="tpu_custom_call" | custom-call | tf_op jit(solution)/shard_map/attention_forward/pallas_call | solution.py:209
  104.5 0.0 copy-start.5
  104.5 0.0 copy-start.21
  104.5 0.8 fusion.26
  105.4 0.3 multiply_reduce_fusion.2
  105.6 0.2 convert_reduce_fusion.2
  105.9 0.2 add_convert_fusion.refs_8_
  106.2 3.4 %multiply_convert_fusion = (bf16[256,4096]{1,0:T(8,128)(2,1)S(1)}, f32[256,4096]{1,0:T(8,128)S(1)}) fusion(f32[4096]{0:T(1024)S(1)} %copy-done.21, bf16[256,1024]{1,0:T(8,128)(2,1)S(1)} %add_convert_fusion.refs_8_, bf16[1024,4096]{1,0:T(8,128)(2,1)S(1)} %copy-done.20), kind=kOutput, calls=%fused_computation.12 | convolution fusion | flops 2157969408 | bytes 15220736 | tf_op jit(solution)/shard_map/dot_general | solution.py:22
  109.7 7.8 %convert_reduce_fusion = (f32[4096]{0:T(1024)S(1)}, bf16[256,4096]{1,0:T(8,128)(2,1)S(1)}) fusion(f32[256,4096]{1,0:T(8,128)S(1)} %get-tuple-element.83, bf16[256,1024]{1,0:T(8,128)(2,1)S(1)} %get-tuple-element.79.refs_7_, bf16[4096,1024]{1,0:T(8,128)(2,1)} %param.26), kind=kOutput, calls=%fused_computation.11 | convolution fusion | flops 2169499648 | bytes 15220736 | tf_op jit(solution)/shard_map/dot_general | solution.py:26
  117.5 0.0 slice-start
  117.5 7.1 %multiply_reduce_fusion = (f32[1024]{0:T(1024)S(1)}, f32[256]{0:T(256)S(1)}, f32[256]{0:T(256)S(1)}, f32[1024]{0:T(1024)S(1)}, f32[256,1024]{1,0:T(8,128)S(1)}) fusion(f32[256,1024]{1,0:T(8,128)S(1)} %get-tuple-element.81, f32[256]{0:T(256)S(1)} %add_rsqrt_fusion, f32[256]{0:T(256)S(1)} %broadcast_multiply_fusion.2, f32[1024]{0:T(1024)S(1)} %copy-done.18, ...), kind=kOutput, calls=%fused_computation.42 | convolution fusion | flops 2149840384 | bytes 12599296 | tf_op jit(solution)/shard_map/dot_general | solution.py:26
  124.7 1.4 convert_reduce_fusion.3
  126.1 0.7 pad_maximum_fusion.refs_19_
  126.8 1.5 fusion.19.refs_0_
  128.4 3.3 %fusion.21 = bf16[1,256,1024]{2,1,0:T(8,128)(2,1)} fusion(f32[256,1024]{1,0:T(8,128)S(1)} %get-tuple-element.81, bf16[256,4096]{1,0:T(8,128)(2,1)S(1)} %get-tuple-element.82.refs_6_, bf16[4096,1024]{1,0:T(8,128)(2,1)S(1)} %bitcast.57, f32[1024]{0:T(1024)S(1)} %copy-done.24), kind=kOutput, calls=%fused_computation.37 | convolution fusion | flops 2148270080 | bytes 12062720 | tf_op jit(solution)/shard_map/dot_general | solution.py:22
  131.6 0.7 broadcast_in_dim.13.refs_20_
  132.3 136.5 %tail.1 = (bf16[256,1024]{1,0:T(8,128)(2,1)}, f32[9,128,256]{2,1,0:T(8,128)}, bf16[32,48,128]{2,1,0:T(8,128)(2,1)}, f32[32,8,128]{2,1,0:T(8,128)}, f32[32,8,128]{2,1,0:T(8,128)}) custom-call(bf16[1024,256]{1,0:T(8,128)(2,1)} %fusion.19.refs_0_, bf16[64,4096]{1,0:T(8,128)(2,1)} %copy-done.2, bf16[64,4096]{1,0:T(8,128)(2,1)} %copy-done.3, ...), custom_call_target="tpu_custom_call" | custom-call | tf_op jit(solution)/shard_map/tail/pallas_call | solution.py:870
  268.8 3.1 %finish.1 = (bf16[256,1024]{1,0:T(8,128)(2,1)}, f32[32,1024]{1,0:T(8,128)}, f32[32,1024]{1,0:T(8,128)}, f32[32,1024]{1,0:T(8,128)}, f32[32,1024]{1,0:T(8,128)}, ...) custom-call(bf16[256,1024]{1,0:T(8,128)(2,1)} %get-tuple-element.50., ...), custom_call_target="tpu_custom_call" | custom-call | tf_op jit(solution)/shard_map/finish/pallas_call | solution.py:932
  (55 shorter events, 0.2 us)
Async XLA Ops:
  7.2 7.8 %copy-start.8 = (bf16[1024,1024]{1,0:T(8,128)(2,1)S(1)}, bf16[1024,1024]{1,0:T(8,128)(2,1)}, u32[]{:S(2)}) copy-start(bf16[1024,1024]{1,0:T(8,128)(2,1)} %param.21) | copy-start | bytes 6291460
  7.2 7.8 %copy-start.22 = (f32[1024]{0:T(1024)S(1)}, f32[1024]{0:T(1024)}, u32[]{:S(2)}) copy-start(f32[1024]{0:T(1024)} %param.27) | copy-start | bytes 12292
  7.2 124.4 %all-gather.2.cloned.1.call-start = ((), (), s32[]{:S(2)}) async-start(), calls=%async_computation | async-start | bytes 8912896 | tf_op jit(solution)/shard_map/all_gather | solution.py:1005
  12.1 5.1 %copy-start.15 = (bf16[256,1024]{1,0:T(8,128)(2,1)S(1)}, bf16[256,1024]{1,0:T(8,128)(2,1)}, u32[]{:S(2)}) copy-start(bf16[256,1024]{1,0:T(8,128)(2,1)} %fusion.25) | copy-start | bytes 1572868
  12.1 5.2 %copy-start.23 = (f32[1024]{0:T(1024)S(1)}, f32[1024]{0:T(1024)}, u32[]{:S(2)}) copy-start(f32[1024]{0:T(1024)} %param.28) | copy-start | bytes 12292
  12.1 5.1 %copy-start.9 = (bf16[1024,1024]{1,0:T(8,128)(2,1)S(1)}, bf16[1024,1024]{1,0:T(8,128)(2,1)}, u32[]{:S(2)}) copy-start(bf16[1024,1024]{1,0:T(8,128)(2,1)} %param.23) | copy-start | bytes 6291460
  15.0 89.4 %copy-start.25 = (s32[1,256]{1,0:T(1,128)S(1)}, s32[1,256]{1,0:T(1,128)}, u32[]{:S(2)}) copy-start(s32[1,256]{1,0:T(1,128)} %param.19) | copy-start | bytes 3076
  15.0 89.5 %copy-start.6 = (bf16[1,256,1024]{2,1,0:T(8,128)(2,1)S(1)}, bf16[1,256,1024]{2,1,0:T(8,128)(2,1)}, u32[]{:S(2)}) copy-start(bf16[1,256,1024]{2,1,0:T(8,128)(2,1)} %param.18) | copy-start | bytes 1572868
  15.0 89.5 %copy-start.13 = (bf16[1024,1024]{1,0:T(8,128)(2,1)S(1)}, bf16[1024,1024]{1,0:T(8,128)(2,1)}, u32[]{:S(2)}) copy-start(bf16[1024,1024]{1,0:T(8,128)(2,1)} %param.24) | copy-start | bytes 6291460
  15.0 89.5 %copy-start.17 = (f32[1024]{0:T(1024)S(1)}, f32[1024]{0:T(1024)}, u32[]{:S(2)}) copy-start(f32[1024]{0:T(1024)} %param.29) | copy-start | bytes 12292
  18.2 87.4 %copy-start.16 = (bf16[1,256,1024]{2,1,0:T(8,128)(2,1)S(1)}, bf16[1,256,1024]{2,1,0:T(8,128)(2,1)}, u32[]{:S(2)}) copy-start(bf16[1,256,1024]{2,1,0:T(8,128)(2,1)} %param.20) | copy-start | bytes 1572868
  18.3 87.6 %copy-start.18 = (f32[1024]{0:T(1024)S(1)}, f32[1024]{0:T(1024)}, u32[]{:S(2)}) copy-start(f32[1024]{0:T(1024)} %param.34) | copy-start | bytes 12292
  18.3 87.6 %copy-start.19 = (f32[1024]{0:T(1024)S(1)}, f32[1024]{0:T(1024)}, u32[]{:S(2)}) copy-start(f32[1024]{0:T(1024)} %param.35) | copy-start | bytes 12292
  18.3 87.9 %copy-start.20 = (bf16[1024,4096]{1,0:T(8,128)(2,1)S(1)}, bf16[1024,4096]{1,0:T(8,128)(2,1)}, u32[]{:S(2)}) copy-start(bf16[1024,4096]{1,0:T(8,128)(2,1)} %param.25) | copy-start | bytes 25165828
  104.4 5.2 %copy-start = (bf16[1024,256]{1,0:T(8,128)(2,1)}, bf16[1024,256]{1,0:T(8,128)(2,1)S(1)}, u32[]{:S(2)}) copy-start(bf16[1024,256]{1,0:T(8,128)(2,1)S(1)} %get-tuple-element.44.refs_10_) | copy-start | bytes 1572868
  104.4 5.2 %copy-start.1 = (f32[64,4096]{1,0:T(8,128)}, f32[64,4096]{1,0:T(8,128)S(1)}, u32[]{:S(2)}) copy-start(f32[64,4096]{1,0:T(8,128)S(1)} %get-tuple-element.48.refs_4_) | copy-start | bytes 3145732
  104.4 5.2 %copy-start.2 = (bf16[64,4096]{1,0:T(8,128)(2,1)}, bf16[64,4096]{1,0:T(8,128)(2,1)S(1)}, u32[]{:S(2)}) copy-start(bf16[64,4096]{1,0:T(8,128)(2,1)S(1)} %get-tuple-element.45.refs_1_) | copy-start | bytes 1572868
  104.5 5.2 %copy-start.3 = (bf16[64,4096]{1,0:T(8,128)(2,1)}, bf16[64,4096]{1,0:T(8,128)(2,1)S(1)}, u32[]{:S(2)}) copy-start(bf16[64,4096]{1,0:T(8,128)(2,1)S(1)} %get-tuple-element.46.refs_2_) | copy-start | bytes 1572868
  104.5 5.2 %copy-start.4 = (bf16[64,4096]{1,0:T(8,128)(2,1)}, bf16[64,4096]{1,0:T(8,128)(2,1)S(1)}, u32[]{:S(2)}) copy-start(bf16[64,4096]{1,0:T(8,128)(2,1)S(1)} %get-tuple-element.47.refs_3_) | copy-start | bytes 1572868
  104.5 5.2 %copy-start.5 = (f32[8,4096]{1,0:T(8,128)}, f32[8,4096]{1,0:T(8,128)S(1)}, u32[]{:S(2)}) copy-start(f32[8,4096]{1,0:T(8,128)S(1)} %get-tuple-element.49.refs_5_) | copy-start | bytes 393220
  104.5 1.7 copy-start.21
  105.9 18.8 %copy-start.7 = (bf16[256,1024]{1,0:T(8,128)(2,1)}, bf16[256,1024]{1,0:T(8,128)(2,1)S(1)}, u32[]{:S(2)}) copy-start(bf16[256,1024]{1,0:T(8,128)(2,1)S(1)} %get-tuple-element.79.refs_7_) | copy-start | bytes 1572868
  106.2 3.5 %copy-start.14 = (bf16[256,1024]{1,0:T(8,128)(2,1)}, bf16[256,1024]{1,0:T(8,128)(2,1)S(1)}, u32[]{:S(2)}) copy-start(bf16[256,1024]{1,0:T(8,128)(2,1)S(1)} %add_convert_fusion.refs_8_) | copy-start | bytes 1572868
  109.7 18.7 %copy-start.10 = (bf16[256,4096]{1,0:T(8,128)(2,1)}, bf16[256,4096]{1,0:T(8,128)(2,1)S(1)}, u32[]{:S(2)}) copy-start(bf16[256,4096]{1,0:T(8,128)(2,1)S(1)} %get-tuple-element.82.refs_6_) | copy-start | bytes 6291460
  117.5 7.2 %copy-start.11 = (bf16[256,4096]{1,0:T(8,128)(2,1)}, bf16[256,4096]{1,0:T(8,128)(2,1)S(1)}, u32[]{:S(2)}) copy-start(bf16[256,4096]{1,0:T(8,128)(2,1)S(1)} %get-tuple-element.86.refs_9_) | copy-start | bytes 6291460
  117.5 10.9 %slice-start = ((s8[8388608]{0:T(1024)(128)(4,1)}), s8[4194304]{0:T(1024)(128)(4,1)S(1)}, s32[]{:S(2)}) async-start(s8[8388608]{0:T(1024)(128)(4,1)} %bitcast.56), calls=%async_computation.1 | async-start | bytes 8388608
  117.5 10.8 %slice-start.1 = ((s8[8388608]{0:T(1024)(128)(4,1)}), s8[4194304]{0:T(1024)(128)(4,1)S(1)}, s32[]{:S(2)}) async-start(s8[8388608]{0:T(1024)(128)(4,1)} %bitcast.56), calls=%async_computation.2 | async-start | bytes 8388608
  124.6 3.7 %copy-start.24 = (f32[1024]{0:T(1024)S(1)}, f32[1024]{0:T(1024)}, u32[]{:S(2)}) copy-start(f32[1024]{0:T(1024)} %param.31) | copy-start | bytes 12292
  126.1 5.5 %copy-start.12 = (bf16[256,1024]{1,0:T(8,128)(2,1)}, bf16[256,1024]{1,0:T(8,128)(2,1)S(1)}, u32[]{:S(2)}) copy-start(bf16[256,1024]{1,0:T(8,128)(2,1)S(1)} %get-tuple-element.76.refs_11_) | copy-start | bytes 1572868
Sparse Core Ops, SparseCore 0:
  12.2 111.3 all-gather.1
